TPU v7x, 128 devices: a whole 4x4x4 slice. The times are simulated.
128 devices in a mesh: seq: 32 (over y, x, core), head: 4 (over z).
Axes of the slice: x: 4, y: 4, z: 4, core: 2. Of those that a mesh axis runs over, the one named last changes fastest.
Arguments:
- queries: bfloat16 [131072, 1024], P('seq', 'head'), may hold values from -720 to 720
- keys: bfloat16 [131072, 1024], P('seq', 'head'), may hold values from -6 to 6
- values: bfloat16 [131072, 1024], P('seq', 'head'), may hold values from -6 to 6
- cluster: int32 [1024, 1], P('seq'), may hold values from 0 to 31; in each aligned block of 32 rows (0 to 31, 32 to 63, ...) at most 2 rows name the same one
- w_out: bfloat16 [1024, 1024], P('head'), may hold values from -0.5 to 0.5
Outputs:
- mixed: bfloat16 [131072, 1024], P('seq', 'head')
Inputs may be any that keep to these rules, and one draw needn't show every extreme that they name: In the 32 blocks of one index of seq no cluster is named more than 2 times, and on some index of seq a cluster is named exactly 2 times.
All inputs are finite; a program needn't handle non-finite values.
Results may differ from a plain program's by a relative error of at most 0.0054.
Values may be sent and summed in bfloat16 or wider, within the bound.
A program may use at most 128 MiB of HBM per device.

v0:
```python
import jax
import jax.numpy as jnp
from jax import lax
from jax.sharding import PartitionSpec as P

HEADS = 16
BLOCK = 128


def body(queries, keys, values, cluster, w_out):
    seq_count = lax.axis_size("seq")
    head_count = lax.axis_size("head")
    seq_index = lax.axis_index("seq")
    tok_rows, feat_width = queries.shape
    block_count = tok_rows // BLOCK
    head_local = HEADS // head_count
    head_size = feat_width // head_local
    slot_depth = max(2, 2 * block_count // seq_count)
    slot_total = seq_count * slot_depth
    score_scale = head_size ** (-0.5)
    all_clusters = lax.all_gather(cluster, "seq", axis=0, tiled=True).reshape(
        seq_count, block_count
    )
    owner_range = jnp.arange(seq_count, dtype=jnp.int32)
    owner_hits = (all_clusters[:, :, None] == owner_range[None, None, :]).astype(jnp.int32)
    slot_rank = jnp.sum(jnp.cumsum(owner_hits, axis=1) * owner_hits, axis=2) - 1
    slot_targets = all_clusters * slot_depth + slot_rank
    my_targets = lax.dynamic_index_in_dim(slot_targets, seq_index, 0, keepdims=False)
    slot_range = jnp.arange(slot_total, dtype=jnp.int32)
    send_match = my_targets[None, :] == slot_range[:, None]
    filled = jnp.any(send_match, axis=1)
    source_block = jnp.argmax(send_match, axis=1)

    def pack_slots(source_array):
        blocks = source_array.reshape(block_count, BLOCK, feat_width)
        placed = jnp.where(
            filled[:, None, None], blocks[source_block], jnp.zeros((), source_array.dtype)
        )
        return placed.reshape(seq_count, slot_depth, BLOCK, feat_width)

    recv_query, recv_key, recv_value = (
        lax.all_to_all(pack_slots(queries), "seq", split_axis=0, concat_axis=0, tiled=True),
        lax.all_to_all(pack_slots(keys), "seq", split_axis=0, concat_axis=0, tiled=True),
        lax.all_to_all(pack_slots(values), "seq", split_axis=0, concat_axis=0, tiled=True),
    )
    owned = all_clusters == seq_index
    depth_range = jnp.arange(slot_depth, dtype=jnp.int32)
    slot_match = owned[:, None, :] & (slot_rank[:, None, :] == depth_range[None, :, None])
    global_block = (
        owner_range[:, None] * block_count + jnp.arange(block_count, dtype=jnp.int32)[None, :]
    )
    block_ids = jnp.where(
        jnp.any(slot_match, axis=2),
        jnp.sum(jnp.where(slot_match, global_block[:, None, :], 0), axis=2),
        -1,
    ).reshape(slot_total)
    occupied = block_ids >= 0
    compact_order = jnp.argsort(jnp.where(occupied, slot_range, slot_range + slot_total))
    restore_order = jnp.argsort(compact_order)
    live_count = jnp.sum(occupied.astype(jnp.int32))
    tile_blocks = min(slot_total, max(1, 512 // BLOCK))
    tile_count = slot_total // tile_blocks
    tile_rows = tile_blocks * BLOCK

    def compact_tiles(received):
        ordered = received.reshape(slot_total, BLOCK, feat_width)[compact_order]
        return ordered.reshape(tile_count, tile_rows, head_local, head_size)

    tile_query = compact_tiles(recv_query)
    tile_key = compact_tiles(recv_key)
    tile_value = compact_tiles(recv_value)
    row_block = jnp.repeat(block_ids[compact_order], BLOCK).reshape(tile_count, tile_rows)
    row_offset = jnp.tile(jnp.arange(BLOCK, dtype=jnp.int32), tile_blocks)
    live_tiles = (live_count + tile_blocks - 1) // tile_blocks

    def query_tile(tile_index, outputs):
        query_part = tile_query[tile_index]
        query_ids = row_block[tile_index]

        def key_tile(key_index, carry):
            running_max, running_sum, accumulated = carry
            key_part = tile_key[key_index]
            value_part = tile_value[key_index]
            key_ids = row_block[key_index]
            scores = (
                jnp.einsum("qhd,khd->hqk", query_part, key_part, preferred_element_type=jnp.float32)
                * score_scale
            )
            permitted = (key_ids[None, :] >= 0) & (
                (key_ids[None, :] < query_ids[:, None])
                | (key_ids[None, :] == query_ids[:, None])
                & (row_offset[None, :] <= row_offset[:, None])
            )
            scores = jnp.where(permitted[None], scores, jnp.float32(-1e30))
            newer_max = jnp.maximum(running_max, jnp.max(scores, axis=2))
            rescale = jnp.exp(running_max - newer_max)
            weights = jnp.exp(scores - newer_max[:, :, None])
            running_sum = running_sum * rescale + jnp.sum(weights, axis=2)
            partial_out = jnp.einsum(
                "hqk,khd->qhd",
                weights.astype(jnp.bfloat16),
                value_part,
                preferred_element_type=jnp.float32,
            )
            accumulated = accumulated * rescale.T[:, :, None] + partial_out
            return (newer_max, running_sum, accumulated)

        initial = (
            jnp.full((head_local, tile_rows), -1e30, jnp.float32),
            jnp.zeros((head_local, tile_rows), jnp.float32),
            jnp.zeros((tile_rows, head_local, head_size), jnp.float32),
        )
        running_max, running_sum, accumulated = lax.fori_loop(0, tile_index + 1, key_tile, initial)
        result = (
            (accumulated / running_sum.T[:, :, None])
            .astype(jnp.bfloat16)
            .reshape(tile_rows, feat_width)
        )
        return lax.dynamic_update_index_in_dim(outputs, result, tile_index, 0)

    attended_slots = lax.fori_loop(
        0, live_tiles, query_tile, jnp.zeros((tile_count, tile_rows, feat_width), jnp.bfloat16)
    )
    answer_slots = attended_slots.reshape(slot_total, BLOCK, feat_width)[restore_order].reshape(
        seq_count, slot_depth, BLOCK, feat_width
    )
    returned = lax.all_to_all(answer_slots, "seq", split_axis=0, concat_axis=0, tiled=True)
    attended = returned.reshape(slot_total, BLOCK, feat_width)[my_targets].reshape(
        tok_rows, feat_width
    )
    partial_proj = jnp.dot(attended, w_out, preferred_element_type=jnp.float32)
    mixed = lax.psum_scatter(partial_proj, "head", scatter_dimension=1, tiled=True)
    return mixed.astype(jnp.bfloat16)


def solution(mesh):
    placed = (P("seq", "head"), P("seq", "head"), P("seq", "head"), P("seq", None), P("head", None))
    return jax.shard_map(
        body, mesh=mesh, in_specs=placed, out_specs=P("seq", "head"), check_vma=False
    )
```

profile of v0, /device:TPU:1, one launch (start us, length us, event | category | flops | bytes accessed | tf_op | source)
XLA Modules:
  0.0 1281.7 jit_solution(18042619007814765252)
XLA Ops:
  9.4 14.4 %all-reduce = s32[1024]{0:T(1024)S(1)} all-reduce(s32[1024]{0:T(1024)S(1)} %bitcast_dynamic-update-slice_fusion), channel_id=1, replica_groups=mesh['seq'=32,'head'=4] {'seq'}, use_global_device_ids=true, to_apply=%add | all-reduce | flops 1024 | bytes 8192
  31.3 2.8 gather_fusion
  34.1 4.5 gather_fusion.3
  38.6 2.7 gather_fusion.5
  41.4 7.2 broadcast_select_fusion
  48.6 58.2 %all_to_all.20 = bf16[32,2,128,256]{3,2,1,0:T(8,128)(2,1)} all-to-all(bf16[32,2,128,256]{3,2,1,0:T(8,128)(2,1)S(1)} %get-tuple-element.214), channel_id=1, replica_groups=mesh['seq'=32,'head'=4] {'seq'}, dimensions={0} | all-to-all | bytes 8388608 | tf_op jit(solution)/shard_map/all_to_all | solution.py:42
  106.8 55.2 %all_to_all.21 = bf16[32,2,128,256]{3,2,1,0:T(8,128)(2,1)} all-to-all(bf16[32,2,128,256]{3,2,1,0:T(8,128)(2,1)S(1)} %get-tuple-element.213), channel_id=1, replica_groups=mesh['seq'=32,'head'=4] {'seq'}, dimensions={0} | all-to-all | bytes 8388608 | tf_op jit(solution)/shard_map/all_to_all | solution.py:43
  162.0 4.8 all-to-all-start.2
  168.5 5.0 gather_fusion.1
  173.5 12.9 %reshape.335 = bf16[16,512,4,64]{3,2,1,0:T(4,128)(2,1)} reshape(bf16[64,128,256]{2,1,0:T(8,128)(2,1)} %gather_fusion.1) | data formatting | bytes 8388608 | tf_op jit(solution)/shard_map/reshape | solution.py:67
  186.4 12.7 copy.52
  199.1 5.0 gather_fusion.4
  204.1 12.9 %reshape.336 = bf16[16,512,4,64]{3,2,1,0:T(4,128)(2,1)} reshape(bf16[64,128,256]{2,1,0:T(8,128)(2,1)} %gather_fusion.4) | data formatting | bytes 8388608 | tf_op jit(solution)/shard_map/reshape | solution.py:67
  216.9 12.7 copy.53
  229.6 4.9 gather_fusion.6
  234.6 12.9 %reshape.337 = bf16[16,512,4,64]{3,2,1,0:T(4,128)(2,1)} reshape(bf16[64,128,256]{2,1,0:T(8,128)(2,1)} %gather_fusion.6) | data formatting | bytes 8388608 | tf_op jit(solution)/shard_map/reshape | solution.py:67
  247.4 12.7 copy.54
  262.5 169.3 %while.27 = (s32[]{:T(128)}, bf16[16,512,256]{2,1,0:T(8,128)(2,1)}, s32[]{:T(128)}, bf16[16,512,4,64]{1,3,2,0:T(8,128)(2,1)}, s32[16,512]{1,0:T(8,128)S(1)}, /*i...) while((s32[]{:T(128)}, bf16[16,512,256]{2,1,0:T(8,128)(2,1)}, ...), condition=%wide.region_13.14_spmd.clone, body=%wide.region_8.13_spmd.clone.sunk | while | flops 282073600 | bytes 18523632 | solution.py:121
  263.6 5.6 while.28
  271.1 11.1 while.28
  284.2 16.6 %while.28 = (s32[]{:T(128)}, f32[4,512]{1,0:T(4,128)S(1)}, f32[4,512]{1,0:T(4,128)S(1)}, f32[512,4,64]{0,2,1:T(8,128)S(1)}, s32[]{:T(128)}, /*index=5*/s32[16,51...) while((s32[]{:T(128)}, f32[4,512]{1,0:T(4,128)S(1)}, ...), condition=%wide.region_12.12_spmd, body=%wide.region_9.11_spmd.sunk | while | flops 281811456 | bytes 15609011 | solution.py:113
  302.9 22.2 %while.28 = (s32[]{:T(128)}, f32[4,512]{1,0:T(4,128)S(1)}, f32[4,512]{1,0:T(4,128)S(1)}, f32[512,4,64]{0,2,1:T(8,128)S(1)}, s32[]{:T(128)}, /*index=5*/s32[16,51...) while((s32[]{:T(128)}, f32[4,512]{1,0:T(4,128)S(1)}, ...), condition=%wide.region_12.12_spmd, body=%wide.region_9.11_spmd.sunk | while | flops 281811456 | bytes 15609011 | solution.py:113
  327.1 27.7 %while.28 = (s32[]{:T(128)}, f32[4,512]{1,0:T(4,128)S(1)}, f32[4,512]{1,0:T(4,128)S(1)}, f32[512,4,64]{0,2,1:T(8,128)S(1)}, s32[]{:T(128)}, /*index=5*/s32[16,51...) while((s32[]{:T(128)}, f32[4,512]{1,0:T(4,128)S(1)}, ...), condition=%wide.region_12.12_spmd, body=%wide.region_9.11_spmd.sunk | while | flops 281811456 | bytes 15609011 | solution.py:113
  356.8 33.3 %while.28 = (s32[]{:T(128)}, f32[4,512]{1,0:T(4,128)S(1)}, f32[4,512]{1,0:T(4,128)S(1)}, f32[512,4,64]{0,2,1:T(8,128)S(1)}, s32[]{:T(128)}, /*index=5*/s32[16,51...) while((s32[]{:T(128)}, f32[4,512]{1,0:T(4,128)S(1)}, ...), condition=%wide.region_12.12_spmd, body=%wide.region_9.11_spmd.sunk | while | flops 281811456 | bytes 15609011 | solution.py:113
  392.1 38.8 %while.28 = (s32[]{:T(128)}, f32[4,512]{1,0:T(4,128)S(1)}, f32[4,512]{1,0:T(4,128)S(1)}, f32[512,4,64]{0,2,1:T(8,128)S(1)}, s32[]{:T(128)}, /*index=5*/s32[16,51...) while((s32[]{:T(128)}, f32[4,512]{1,0:T(4,128)S(1)}, ...), condition=%wide.region_12.12_spmd, body=%wide.region_9.11_spmd.sunk | while | flops 281811456 | bytes 15609011 | solution.py:113
  431.8 4.9 gather_fusion.7
  436.8 624.0 %all-to-all-start.3 = ((bf16[32,2,128,256]{3,2,1,0:T(8,128)(2,1)}), bf16[32,2,128,256]{3,2,1,0:T(8,128)(2,1)}, u32[]{:S(2)}, u32[]{:S(2)}) async-start(bf16[32,2,128,256]{3,2,1,0:T(8,128)(2,1)} %bitcast.93), calls=%async_computation.3 | async-start | bytes 8388608 | tf_op jit(solution)/shard_map/all_to_all | solution.py:127
  1060.9 50.6 %all-to-all-done.3 = bf16[32,2,128,256]{3,2,1,0:T(8,128)(2,1)} async-done(((bf16[32,2,128,256]{3,2,1,0:T(8,128)(2,1)}), bf16[32,2,128,256]{3,2,1,0:T(8,128)(2,1)}, u32[]{:S(2)}, u32[]{:S(2)}) %all-to-all-start.3) | async-done | bytes 4194336 | tf_op jit(solution)/shard_map/all_to_all | solution.py:127
  1111.5 2.9 gather_fusion.8
  1114.4 8.1 fusion.33
  1122.4 148.7 %reduce-scatter.2.cloned.1.call-done = f32[4096,256]{1,0:T(8,128)} async-done(((f32[4096,1024]{1,0:T(8,128)}), f32[4096,256]{1,0:T(8,128)}) %reduce-scatter.2.cloned.1.call-update) | async-done | bytes 4194320 | tf_op jit(solution)/shard_map/reduce_scatter | solution.py:132
  1271.2 3.7 convert_element_type.18
  (339 shorter events, 180.2 us)
Async XLA Ops:
  6.5 24.7 %copy-start = (bf16[4096,256]{1,0:T(8,128)(2,1)S(1)}, bf16[4096,256]{1,0:T(8,128)(2,1)}, u32[]{:S(2)}) copy-start(bf16[4096,256]{1,0:T(8,128)(2,1)} %param.9) | copy-start | bytes 6291460
  25.1 0.6 copy-start.4
  34.1 4.5 copy-start.2
  162.0 67.6 %all-to-all-start.2 = ((bf16[32,2,128,256]{3,2,1,0:T(8,128)(2,1)}), bf16[32,2,128,256]{3,2,1,0:T(8,128)(2,1)}, u32[]{:S(2)}, u32[]{:S(2)}) async-start(bf16[32,2,128,256]{3,2,1,0:T(8,128)(2,1)} %get-tuple-element.212), calls=%async_computation.2 | async-start | bytes 8388608 | tf_op jit(solution)/shard_map/all_to_all | solution.py:44
  436.8 624.1 %copy-start.5 = (s32[32]{0:T(128)S(1)}, s32[32]{0:T(128)}, u32[]{:S(2)}) copy-start(s32[32]{0:T(128)} %copy-done.4) | copy-start | bytes 388
  436.8 674.7 %all-to-all-start.3 = ((bf16[32,2,128,256]{3,2,1,0:T(8,128)(2,1)}), bf16[32,2,128,256]{3,2,1,0:T(8,128)(2,1)}, u32[]{:S(2)}, u32[]{:S(2)}) async-start(bf16[32,2,128,256]{3,2,1,0:T(8,128)(2,1)} %bitcast.93), calls=%async_computation.3 | async-start | bytes 8388608 | tf_op jit(solution)/shard_map/all_to_all | solution.py:127
  1060.8 53.6 %copy-start.3 = (bf16[256,1024]{1,0:T(8,128)(2,1)S(1)}, bf16[256,1024]{1,0:T(8,128)(2,1)}, u32[]{:S(2)}) copy-start(bf16[256,1024]{1,0:T(8,128)(2,1)} %param.13) | copy-start | bytes 1572868
  1060.8 210.4 %reduce-scatter.2.cloned.1.call-start = ((), (), s32[]{:S(2)}) async-start(), calls=%async_computation.5 | async-start | bytes 20971520 | tf_op jit(solution)/shard_map/reduce_scatter | solution.py:132
  1122.4 152.4 %copy-start.1 = (bf16[4096,256]{1,0:T(8,128)(2,1)S(1)}, bf16[4096,256]{1,0:T(8,128)(2,1)}, u32[]{:S(2)}) copy-start(bf16[4096,256]{1,0:T(8,128)(2,1)} %param.9) | copy-start | bytes 6291460
Sparse Core Ops, SparseCore 0:
  1122.6 148.5 reduce-scatter.1
where the time goes:
time: 1290 us; the launch traced here: 1280 us
  starting transfers between devices  629 us (49%)
  waiting for transfers between devices  199 us (15%)
  local copies, waits for them, and re-layouts  129 us (10%)
  blocking collectives  128 us (10%)
  matrix products  124 us (10%)
  other arithmetic  55.3 us (4%)
  between operations  14.9 us (1%)
    all_to_all x1, starting transfers between devices, body(): lax.all_to_all(answer_slots, 'seq', split_axis=0, concat_axis=0, tiled=True)  624 us
    reduce_scatter x1, waiting for transfers between devices, body(): lax.psum_scatter(partial_proj, 'head', scatter_dimension=1, tiled=True)  149 us
    dot_general x28, matrix products, key_tile(): jnp.einsum('hqk,khd->qhd', weights.astype(jnp.bfloat16), value_part, pref...  64.3 us
    all_to_all x1, blocking collectives, body(): lax.all_to_all(pack_slots(queries), 'seq', split_axis=0, concat_axis=0, t...  58.2 us
    all_to_all x1, blocking collectives, body(): lax.all_to_all(pack_slots(keys), 'seq', split_axis=0, concat_axis=0, tile...  55.2 us
    dot_general x28, matrix products, key_tile(): jnp.einsum('qhd,khd->hqk', query_part, key_part, preferred_element_type=j...  52 us
    all_to_all x1, waiting for transfers between devices, body(): lax.all_to_all(answer_slots, 'seq', split_axis=0, concat_axis=0, tiled=True)  50.6 us
    unnamed x19, local copies, waits for them, and re-layouts  40.3 us
  transfers between devices with their start and end apart: 3, of which 2 were waited for; matrix products, arithmetic and copies ran while one was open for 5% of the time, Pallas kernels for 0%

commit v1 on v0

v1 whole, which is shorter than its diff:
```python
import functools

import jax
import jax.numpy as jnp
from jax import lax
from jax.experimental import pallas as pl
from jax.experimental.pallas import tpu as pltpu
from jax.sharding import PartitionSpec as P

HEADS = 16
BLOCK = 128
HEAD = 64
MAIN = 5
FULL = 8
TILE = 4
NT = (((1,), (1,)), ((), ()))


def tables(cluster):
    n = lax.axis_size("seq")
    me = lax.axis_index("seq")
    blocks = cluster.shape[0]
    mine = cluster.reshape(blocks)
    everyone = lax.all_to_all(
        jnp.broadcast_to(mine[None, :], (n, blocks)), "seq", split_axis=0, concat_axis=0, tiled=True
    )
    ids = jnp.arange(n, dtype=jnp.int32)
    heads = jnp.arange(4, dtype=jnp.int32)
    counts = jnp.sum((everyone[:, :, None] == ids).astype(jnp.int32), axis=1)
    weight = jnp.max(counts, axis=0)
    before = ids[None, :] < ids[:, None]
    rank2 = jnp.sum((before & (weight == 2)[None, :]).astype(jnp.int32), axis=1)
    rank1 = jnp.sum((before & (weight == 1)[None, :]).astype(jnp.int32), axis=1)
    twos = 4 * jnp.sum((weight == 2).astype(jnp.int32))
    full, rem = twos // n, twos % n
    light = n - rem
    heavy = jnp.maximum(rem, 1)
    k2 = rank2[:, None] * 4 + heads
    k = rank1[:, None] * 4 + heads
    a = jnp.maximum(MAIN - 2 * full, 0) * light
    b = jnp.maximum(MAIN - 2 - 2 * full, 0) * rem
    c0 = jnp.maximum(MAIN, 2 * full)
    c = (FULL - c0) * light
    kb, kc = k - a, k - a - b
    kd = kc - c
    owner1 = jnp.where(
        k < a, rem + k % light, jnp.where(kb < b, kb % heavy, jnp.where(kc < c, rem + kc % light, kd % heavy))
    )
    slot1 = jnp.where(
        k < a,
        2 * full + k // light,
        jnp.where(
            kb < b,
            2 * full + 2 + kb // heavy,
            jnp.where(kc < c, c0 + kc // light, jnp.maximum(MAIN, 2 * full + 2) + kd // heavy),
        ),
    )
    two = (weight == 2)[:, None]
    used = (weight > 0)[:, None]
    owner = jnp.where(two, k2 % n, owner1)
    slot = jnp.where(two, 2 * (k2 // n), slot1)
    fits = jnp.all(~used | (slot + weight[:, None] <= MAIN))
    hit = mine[:, None] == ids[None, :]
    earlier = jnp.arange(blocks)[None, :] < jnp.arange(blocks)[:, None]
    second = jnp.sum((earlier & (mine[None, :] == mine[:, None])).astype(jnp.int32), axis=1)
    target = jnp.sum(jnp.where(hit[:, :, None], (owner * FULL + slot)[None], 0), axis=1) + second[:, None]
    slots = jnp.arange(FULL, dtype=jnp.int32)
    held = (used & (owner == me))[None] & (slot[None] == slots[:, None, None])
    unit = jnp.sum(jnp.where(held, weight[None, :, None], 0), axis=(1, 2))
    count = jnp.sum(jnp.where(jnp.any(held, axis=2)[:, None, :], counts[None], 0), axis=2)
    return fits, target.reshape(blocks * 4), unit, count.reshape(FULL * n)


PACK = 4


def pack_kernel(target, q_ref, k_ref, v_ref, out_ref, stage, eye, sems):
    step = pl.program_id(0)
    par = lax.rem(step, 2)

    @pl.when(step == 0)
    def _():
        r = lax.broadcasted_iota(jnp.int32, (256, 256), 0)
        c = lax.broadcasted_iota(jnp.int32, (256, 256), 1)
        eye[...] = jnp.where(r == c, 1.0, 0.0).astype(jnp.bfloat16)

    def copy(at, p, i):
        t = target[at * (PACK * 4) + i]
        return pltpu.make_async_copy(
            stage.at[p, i], out_ref.at[lax.div(t, FULL), lax.rem(t, FULL)], sems.at[p, i]
        )

    @pl.when(step >= 2)
    def _():
        for i in range(PACK * 4):
            copy(step - 2, par, i).wait()

    lane = lax.broadcasted_iota(jnp.int32, (BLOCK, 128), 1)
    for t in range(PACK):
        rows = slice(t * BLOCK, (t + 1) * BLOCK)
        vt = lax.dot_general(eye[...], v_ref[rows, :], NT, preferred_element_type=jnp.float32)
        vt = vt.astype(jnp.bfloat16)
        for pair in range(2):
            cols = slice(pair * 128, (pair + 1) * 128)
            q = q_ref[rows, cols].astype(jnp.float32)
            k = k_ref[rows, cols].astype(jnp.float32)
            even = jnp.where(lane < HEAD, q, pltpu.roll(k, HEAD, 1))
            odd = jnp.where(lane < HEAD, pltpu.roll(q, HEAD, 1), k)
            stage[par, t * 4 + pair * 2, 0:BLOCK, :] = even.astype(jnp.bfloat16)
            stage[par, t * 4 + pair * 2 + 1, 0:BLOCK, :] = odd.astype(jnp.bfloat16)
        for h in range(4):
            stage[par, t * 4 + h, BLOCK : BLOCK + HEAD, :] = vt[h * HEAD : (h + 1) * HEAD]
    for i in range(PACK * 4):
        copy(step, par, i).start()

    @pl.when(step == pl.num_programs(0) - 1)
    def _():
        for i in range(PACK * 4):
            copy(step - 1, 1 - par, i).wait()
        for i in range(PACK * 4):
            copy(step, par, i).wait()


def pack(target, queries, keys, values, n, depth):
    rows, width = queries.shape
    tile = pl.BlockSpec((PACK * BLOCK, width), lambda i, *_: (i, 0))
    return pl.pallas_call(
        pack_kernel,
        out_shape=jax.ShapeDtypeStruct((n, depth, BLOCK + HEAD, 128), jnp.bfloat16),
        grid_spec=pltpu.PrefetchScalarGridSpec(
            num_scalar_prefetch=1,
            grid=(rows // (PACK * BLOCK),),
            in_specs=[tile, tile, tile],
            out_specs=pl.BlockSpec(memory_space=pl.ANY),
            scratch_shapes=[
                pltpu.VMEM((2, PACK * 4, BLOCK + HEAD, 128), jnp.bfloat16),
                pltpu.VMEM((256, 256), jnp.bfloat16),
                pltpu.SemaphoreType.DMA((2, PACK * 4)),
            ],
        ),
        name=f"pack{depth}",
    )(target, queries, keys, values)


def attend_kernel(depth, n, unit, count, recv, out, kq, vt, stage, where_from, sizes, pending, in_sems, out_sems):
    tq = TILE * BLOCK

    def fetch(pos, s, j, u):
        at = pl.multiple_of(pos * BLOCK, BLOCK)
        return (
            pltpu.make_async_copy(
                recv.at[s, j, pl.ds(0, BLOCK), :], kq.at[pl.ds(at, BLOCK), :], in_sems.at[u, 0]
            ),
            pltpu.make_async_copy(
                recv.at[s, j, pl.ds(BLOCK, HEAD), :],
                vt.at[pl.ds(0, HEAD), pl.ds(at, BLOCK)],
                in_sems.at[u, 1],
            ),
        )

    def fetch_unit(u, base):
        w = unit[u]

        def source(s, pos):
            here = jnp.where(w > 0, count[u * n + s], 0)
            for r in range(2):

                @pl.when(here > r)
                def _():
                    where_from[pos + r] = s * depth + u + r
                    for c in fetch(pos + r, s, u + r, u):
                        c.start()

            return pos + here

        end = lax.fori_loop(0, n, source, base)
        sizes[u] = end - base
        stop = lax.div(end + TILE - 1, TILE) * TILE

        def blank(pos, c):
            at = pl.multiple_of(pos * BLOCK, BLOCK)
            vt[0:HEAD, pl.ds(at, BLOCK)] = jnp.zeros((HEAD, BLOCK), jnp.bfloat16)
            return c

        lax.fori_loop(end, stop, blank, 0)
        return stop

    lax.fori_loop(0, depth, fetch_unit, 0)
    ones = lax.broadcasted_iota(jnp.int32, (16, vt.shape[1]), 0)
    vt[HEAD : HEAD + 16, :] = jnp.where(ones == 0, 1.0, 0.0).astype(jnp.bfloat16)
    for p in range(2):
        for t in range(TILE):
            pending[p * TILE + t] = 0

    lane = lax.broadcasted_iota(jnp.int32, (tq, 128), 1)
    krow = lax.broadcasted_iota(jnp.int32, (tq, tq), 0)
    qcol = lax.broadcasted_iota(jnp.int32, (tq, tq), 1)
    er = lax.broadcasted_iota(jnp.int32, (BLOCK, BLOCK), 0)
    ec = lax.broadcasted_iota(jnp.int32, (BLOCK, BLOCK), 1)
    eye = jnp.where(er == ec, 1.0, 0.0).astype(jnp.bfloat16)
    low = ec < HEAD

    def put(p, t, pos):
        f = where_from[pos]
        return pltpu.make_async_copy(
            stage.at[p, t],
            out.at[pl.ds(lax.div(f, depth) * 4, 4), lax.rem(f, depth)],
            out_sems.at[p, t],
        )

    def run_unit(u, carry):
        base, turn = carry
        size = sizes[u]

        def arrive(i, c):
            for cp in fetch(0, 0, 0, u):
                cp.wait()
            return c

        lax.fori_loop(0, size, arrive, 0)

        def q_tile(i, turn):
            q0 = pl.multiple_of((base + i * TILE) * BLOCK, tq)
            x = kq[pl.ds(q0, tq), :].astype(jnp.float32)
            q = jnp.where(lane >= HEAD, pltpu.roll(x, HEAD, 1) * 0.125, 0.0).astype(jnp.bfloat16)

            def k_tile(at, top, acc, masked):
                at = pl.multiple_of(at, tq)
                s = lax.dot_general(kq[pl.ds(at, tq), :], q, NT, preferred_element_type=jnp.float32)
                if masked:
                    s = jnp.where(krow <= qcol, s, -1e30)
                newer = jnp.maximum(top, jnp.max(s, axis=0, keepdims=True))
                weights = jnp.exp(s - newer).astype(jnp.bfloat16)
                part = jnp.dot(vt[:, pl.ds(at, tq)], weights, preferred_element_type=jnp.float32)
                return newer, acc * jnp.exp(top - newer) + part

            def step(j, c):
                return k_tile((base + j * TILE) * BLOCK, c[0], c[1], False)

            top, acc = lax.fori_loop(
                0,
                i,
                step,
                (jnp.full((1, tq), -1e30, jnp.float32), jnp.zeros((HEAD + 16, tq), jnp.float32)),
            )
            top, acc = k_tile(q0, top, acc, True)
            o = (acc[0:HEAD] / acc[HEAD : HEAD + 1]).astype(jnp.bfloat16)
            p = lax.rem(turn, 2)
            for t in range(TILE):
                pos = base + i * TILE + t

                @pl.when(pending[p * TILE + t] == 1)
                def _():
                    put(p, t, base).wait()

                piece = o[:, t * BLOCK : (t + 1) * BLOCK]
                both = jnp.concatenate([piece, piece], axis=0)
                flat = lax.dot_general(eye, both, NT, preferred_element_type=jnp.float32)
                packed = jnp.where(low[0:HEAD], flat[0:HEAD], flat[HEAD:BLOCK]).astype(jnp.bfloat16)
                stage[p, t] = packed.reshape(4, 16, 128)
                live = i * TILE + t < size
                pending[p * TILE + t] = live.astype(jnp.int32)

                @pl.when(live)
                def _():
                    put(p, t, pos).start()

            return turn + 1

        tiles = lax.div(size + TILE - 1, TILE)
        turn = lax.fori_loop(0, tiles, q_tile, turn)
        return base + tiles * TILE, turn

    lax.fori_loop(0, depth, run_unit, (0, 0))
    for p in range(2):
        for t in range(TILE):

            @pl.when(pending[p * TILE + t] == 1)
            def _():
                put(p, t, 0).wait()


def attend(unit, count, recv):
    n, depth = recv.shape[:2]
    room = depth * n + depth * (TILE - 1)
    room = -(-room // TILE) * TILE
    smem = pl.BlockSpec(memory_space=pltpu.SMEM)
    return pl.pallas_call(
        functools.partial(attend_kernel, depth, n),
        out_shape=jax.ShapeDtypeStruct((n * 4, depth, 16, 128), jnp.bfloat16),
        in_specs=[smem, smem, pl.BlockSpec(memory_space=pl.ANY)],
        out_specs=pl.BlockSpec(memory_space=pl.ANY),
        scratch_shapes=[
            pltpu.VMEM((room * BLOCK, 128), jnp.bfloat16),
            pltpu.VMEM((HEAD + 16, room * BLOCK), jnp.bfloat16),
            pltpu.VMEM((2, TILE, 4, 16, 128), jnp.bfloat16),
            pltpu.SMEM((room + 4,), jnp.int32),
            pltpu.SMEM((depth,), jnp.int32),
            pltpu.SMEM((2 * TILE,), jnp.int32),
            pltpu.SemaphoreType.DMA((depth, 2)),
            pltpu.SemaphoreType.DMA((2, TILE)),
        ],
        compiler_params=pltpu.CompilerParams(vmem_limit_bytes=60 * 2**20),
        name=f"attend{depth}",
    )(unit, count, recv)


PROJ = 8


def project_kernel(target, got, w_ref, out_ref, att):
    step = pl.program_id(0)
    lane = lax.broadcasted_iota(jnp.int32, (16, 128), 1)
    for t in range(PROJ):
        for pair in range(2):
            at = (step * PROJ + t) * 4 + pair * 2
            ea, eb = target[at], target[at + 1]
            for z in range(4):
                even = got[lax.div(ea, FULL) * 4 + z, lax.rem(ea, FULL)].astype(jnp.float32)
                odd = got[lax.div(eb, FULL) * 4 + z, lax.rem(eb, FULL)].astype(jnp.float32)
                cols = slice(z * 256 + pair * 128, z * 256 + pair * 128 + 128)
                lo = jnp.where(lane < HEAD, even, pltpu.roll(odd, HEAD, 1))
                hi = jnp.where(lane < HEAD, pltpu.roll(even, HEAD, 1), odd)
                att[t * 32 : t * 32 + 16, cols] = lo.astype(jnp.bfloat16)
                att[t * 32 + 16 : t * 32 + 32, cols] = hi.astype(jnp.bfloat16)
    mixed = jnp.zeros((PROJ * 32, 1024), jnp.float32)
    for z in range(4):
        mixed += jnp.dot(att[:, z * 256 : (z + 1) * 256], w_ref[z], preferred_element_type=jnp.float32)
    mixed = mixed.astype(jnp.bfloat16)
    for z in range(4):
        out_ref[z] = mixed[:, z * 256 : (z + 1) * 256].reshape(PROJ, 2, 16, 256)


def project(target, got, w_full, blocks):
    return pl.pallas_call(
        project_kernel,
        out_shape=jax.ShapeDtypeStruct((4, blocks, 2, 16, 256), jnp.bfloat16),
        grid_spec=pltpu.PrefetchScalarGridSpec(
            num_scalar_prefetch=1,
            grid=(blocks // PROJ,),
            in_specs=[
                pl.BlockSpec(got.shape, lambda i, *_: (0, 0, 0, 0)),
                pl.BlockSpec(w_full.shape, lambda i, *_: (0, 0, 0)),
            ],
            out_specs=pl.BlockSpec((4, PROJ, 2, 16, 256), lambda i, *_: (0, i, 0, 0, 0)),
            scratch_shapes=[pltpu.VMEM((PROJ * 32, 1024), jnp.bfloat16)],
        ),
        name=f"project{got.shape[1]}",
    )(target, got, w_full)


def route(depth, target, unit, count, queries, keys, values, w_full):
    n = lax.axis_size("seq")
    blocks = queries.shape[0] // BLOCK
    sent = pack(target, queries, keys, values, n, depth)
    recv = lax.all_to_all(sent, "seq", split_axis=0, concat_axis=0, tiled=True)
    answers = attend(unit, count, recv)
    got = lax.all_to_all(answers, ("seq", "head"), split_axis=0, concat_axis=0, tiled=True)
    mixed = project(target, got, w_full, blocks)
    back = lax.all_to_all(mixed, "head", split_axis=0, concat_axis=0, tiled=True)
    return back.transpose(1, 2, 0, 3, 4).reshape(queries.shape)


def body(queries, keys, values, cluster, w_out):
    fits, target, unit, count = tables(cluster)
    w_full = lax.all_to_all(
        jnp.broadcast_to(w_out[None], (4,) + w_out.shape), "head", split_axis=0, concat_axis=0, tiled=True
    )
    return lax.cond(
        fits,
        functools.partial(route, MAIN),
        functools.partial(route, FULL),
        target,
        unit,
        count,
        queries,
        keys,
        values,
        w_full,
    )


def solution(mesh):
    placed = (P("seq", "head"), P("seq", "head"), P("seq", "head"), P("seq", None), P("head", None))
    return jax.shard_map(
        body, mesh=mesh, in_specs=placed, out_specs=P("seq", "head"), check_vma=False
    )
```

time: 1290 us -> 397 us (0.31)
  starting transfers between devices: 629 us -> 11.4 us
  Pallas kernels: 0 us -> 168 us
  matrix products: 124 us -> 0 us
  local copies, waits for them, and re-layouts: 129 us -> 6.37 us
  waiting for transfers between devices: 199 us -> 114 us
  other arithmetic: 55.3 us -> 3.67 us
  blocking collectives: 128 us -> 91.2 us
  between operations: 14.9 us -> 1.51 us
    all_to_all x2, starting transfers between devices: 629 us -> 11.4 us  [the longest x1 6.26 us: route(): recv = lax.all_to_all(sent, 'seq', split_axis=0, concat_axis=0, tiled=True)]
    pallas_call x0 -> x3, Pallas kernels: none -> 168 us  [the longest x1 152 us: attend(): pl.pallas_call(functools.partial(attend_kernel, depth, n), out_shape=jax....]
    reduce_scatter x1 -> x0, waiting for transfers between devices: 149 us -> none  [body(): lax.psum_scatter(partial_proj, 'head', scatter_dimension=1, tiled=True)]
    dot_general x57 -> x0, matrix products: 124 us -> none  [the longest x28 64.3 us: key_tile(): jnp.einsum('hqk,khd->qhd', weights.astype(jnp.bfloat16), value_part, pref...]
    all_to_all x2, waiting for transfers between devices: 50.6 us -> 114 us  [the longest x1 92.2 us: route(): recv = lax.all_to_all(sent, 'seq', split_axis=0, concat_axis=0, tiled=True)]
    unnamed x19 -> x4, local copies, waits for them, and re-layouts: 40.3 us -> 1.32 us
    reshape x5 -> x1, local copies, waits for them, and re-layouts: 38.8 us -> 0.64 us  [tables(): return (fits, target.reshape(blocks * 4), unit, count.reshape(FULL * n))]
    gather x9 -> x0, local copies, waits for them, and re-layouts: 33.5 us -> none  [the longest x3 14.9 us: compact_tiles(): ordered = received.reshape(slot_total, BLOCK, feat_width)[compact_order]]
  transfers between devices with their start and end apart: 3 -> 2, of which waited for: 2 -> 2; matrix products, arithmetic and copies ran while one was open for 5% -> 1% of each run, Pallas kernels for 0% -> 0%
where the time goes in v1:
time: 397 us; the launch traced here: 396 us
  Pallas kernels  168 us (42%)
  waiting for transfers between devices  114 us (29%)
  blocking collectives  91.2 us (23%)
  starting transfers between devices  11.4 us (3%)
  local copies, waits for them, and re-layouts  6.37 us (2%)
    pallas_call x1, Pallas kernels, attend(): pl.pallas_call(functools.partial(attend_kernel, depth, n), out_shape=jax....  152 us
    all_to_all x1, waiting for transfers between devices, route(): recv = lax.all_to_all(sent, 'seq', split_axis=0, concat_axis=0, tiled=True)  92.2 us
    all_to_all x1, blocking collectives, route(): lax.all_to_all(answers, ('seq', 'head'), split_axis=0, concat_axis=0, til...  46.2 us
    all_to_all x1, blocking collectives, route(): lax.all_to_all(mixed, 'head', split_axis=0, concat_axis=0, tiled=True)  29.7 us
    all_to_all x1, waiting for transfers between devices, body(): lax.all_to_all(jnp.broadcast_to(w_out[None], (4,) + w_out.shape), 'head',...  21.7 us
    all_to_all x1, blocking collectives, tables(): lax.all_to_all(jnp.broadcast_to(mine[None, :], (n, blocks)), 'seq', split...  15.3 us
    pallas_call x1, Pallas kernels, pack(): pl.pallas_call(pack_kernel, out_shape=jax.ShapeDtypeStruct((n, depth, BLO...  9.61 us
  transfers between devices with their start and end apart: 2, of which 2 were waited for; matrix products, arithmetic and copies ran while one was open for 1% of the time, Pallas kernels for 0%

profile of v1, /device:TPU:1, one launch (start us, length us, event | category | flops | bytes accessed | tf_op | source)
XLA Modules:
  0.0 396.3 jit_solution(2958064791958408596)
XLA Ops:
  0.0 0.7 broadcast_in_dim.72
  0.7 15.3 %all_to_all.39 = s32[32,1,32]{2,1,0:T(1,128)S(1)} all-to-all(s32[32,1,32]{2,1,0:T(1,128)S(1)} %broadcast_in_dim.72), channel_id=1, replica_groups=mesh['seq'=32,'head'=4] {'seq'}, dimensions={0} | all-to-all | bytes 8192 | tf_op jit(solution)/shard_map/all_to_all | solution.py:24
  16.0 2.6 broadcast_in_dim.115
  18.6 0.0 copy-start.1
  18.6 5.2 %all-to-all-start.7 = ((bf16[4,256,1024]{2,1,0:T(8,128)(2,1)}), bf16[4,256,1024]{2,1,0:T(8,128)(2,1)S(1)}, u32[]{:S(2)}, u32[]{:S(2)}) async-start(bf16[4,256,1024]{2,1,0:T(8,128)(2,1)} %broadcast_in_dim.115), calls=%async_computation.7 | async-start | bytes 4194304 | tf_op jit(solution)/shard_map/all_to_all | solution.py:366
  23.8 0.0 copy-done.1
  23.8 0.1 fusion.3
  23.9 0.2 convert_reduce_fusion
  24.1 0.7 convert_reduce_fusion.3
  25.6 0.1 convert_reduce_fusion.1
  25.8 0.9 fusion.40
  27.4 0.2 fusion.6
  27.6 21.7 %all-to-all-done.7 = bf16[4,256,1024]{2,1,0:T(8,128)(2,1)S(1)} async-done(((bf16[4,256,1024]{2,1,0:T(8,128)(2,1)}), bf16[4,256,1024]{2,1,0:T(8,128)(2,1)S(1)}, u32[]{:S(2)}, u32[]{:S(2)}) %all-to-all-start.7) | async-done | bytes 2097184 | tf_op jit(solution)/shard_map/all_to_all | solution.py:366
  49.3 0.1 eq.105
  49.4 345.6 %conditional.1 = (bf16[4096,256]{1,0:T(8,128)(2,1)S(1)}) conditional(s32[]{:T(128)} %convert_element_type.22, (s32[32,32]{1,0:T(8,128)S(1)}, bf16[4096,256]{1,0:T(8,128)(2,1)}, bf16[4096,256]{1,0:T(8,128)(2,1)}, bf16[4096,256]{1,0:T(8,128)(2,1)}, pred[32]{0:T(512)(128)(4,1)S(1)}, /*index=5*/s32[32,4]{0,1:T(4,128)S(1)}, ...), branch_computations={%region_11.12_spmd, %region_12.13_spmd} | conditional | flops 31704 | bytes 54561548 | solution.py:369
  49.4 0.1 reduce_sum.87
  49.5 0.1 select_reduce_fusion.4
  49.7 0.1 copy.26
  49.8 0.7 add.288.target
  50.4 9.6 %pack5.1 = bf16[32,5,192,128]{3,2,1,0:T(8,128)(2,1)} custom-call(s32[128]{0:T(128)} %add.288.target, bf16[4096,256]{1,0:T(8,128)(2,1)} %get-tuple-element.70.q_ref, bf16[4096,256]{1,0:T(8,128)(2,1)} %get-tuple-element.72.k_ref, bf16[4096,256]{1,0:T(8,128)(2,1)} %get-tuple-element.74.v_ref), custom_call_target="tpu_custom_call" | custom-call | tf_op jit(solution)/shard_map/cond/branch_1_fun/pack5/pallas_call | solution.py:127
  60.0 6.3 %all-to-all-start.3 = ((bf16[32,5,192,128]{3,2,1,0:T(8,128)(2,1)}), bf16[32,5,192,128]{3,2,1,0:T(8,128)(2,1)}, u32[]{:S(2)}, u32[]{:S(2)}) async-start(bf16[32,5,192,128]{3,2,1,0:T(8,128)(2,1)} %pack5.1), calls=%async_computation.3 | async-start | bytes 15728640 | tf_op jit(solution)/shard_map/cond/branch_1_fun/all_to_all | solution.py:356
  66.3 0.2 select_reduce_fusion.3
  66.6 0.6 reshape.352.count
  67.2 0.8 select_reduce_fusion.5.unit
  68.0 92.2 %all-to-all-done.3.recv = bf16[32,5,192,128]{3,2,1,0:T(8,128)(2,1)} async-done(((bf16[32,5,192,128]{3,2,1,0:T(8,128)(2,1)}), bf16[32,5,192,128]{3,2,1,0:T(8,128)(2,1)}, u32[]{:S(2)}, u32[]{:S(2)}) %all-to-all-start.3) | async-done | bytes 7864352 | tf_op jit(solution)/shard_map/cond/branch_1_fun/all_to_all | solution.py:356
  160.3 151.7 %attend5.1 = bf16[128,5,16,128]{3,2,1,0:T(8,128)(2,1)} custom-call(s32[8]{0:T(128)} %select_reduce_fusion.5.unit, s32[256]{0:T(256)} %reshape.352.count, bf16[32,5,192,128]{3,2,1,0:T(8,128)(2,1)} %all-to-all-done.3.recv), custom_call_target="tpu_custom_call" | custom-call | tf_op jit(solution)/shard_map/cond/branch_1_fun/attend5/pallas_call | solution.py:288
  311.9 46.2 %all_to_all.37.got = bf16[128,5,16,128]{3,2,1,0:T(8,128)(2,1)} all-to-all(bf16[128,5,16,128]{3,2,1,0:T(8,128)(2,1)} %attend5.1), channel_id=1, replica_groups=mesh['seq'=32,'head'=4] {'seq','head'}, dimensions={0} | all-to-all | bytes 5242880 | tf_op jit(solution)/shard_map/cond/branch_1_fun/all_to_all | solution.py:358
  358.1 6.9 %project5.1 = bf16[4,32,2,16,256]{4,3,2,1,0:T(8,128)(2,1)} custom-call(s32[128]{0:T(128)} %add.288.target, bf16[128,5,16,128]{3,2,1,0:T(8,128)(2,1)} %all_to_all.37.got, bf16[4,256,1024]{2,1,0:T(8,128)(2,1)S(1)} %get-tuple-element.49.w_ref), custom_call_target="tpu_custom_call" | custom-call | tf_op jit(solution)/shard_map/cond/branch_1_fun/project5/pallas_call | solution.py:335
  365.0 29.7 %all_to_all.38 = bf16[4,32,2,16,256]{4,3,2,1,0:T(8,128)(2,1)S(1)} all-to-all(bf16[4,32,2,16,256]{4,3,2,1,0:T(8,128)(2,1)} %project5.1), channel_id=1, replica_groups=mesh['seq'=32,'head'=4] {'head'}, dimensions={0} | all-to-all | bytes 4194304 | tf_op jit(solution)/shard_map/cond/branch_1_fun/all_to_all | solution.py:360
  394.7 0.3 copy.27
  395.0 0.0 copy-start
  395.0 1.3 copy-done
  (11 shorter events, 0.1 us)
Async XLA Ops:
  18.6 5.2 %copy-start.1 = (s32[32,1]{0,1:T(1,128)S(1)}, s32[32,1]{0,1:T(1,128)}, u32[]{:S(2)}) copy-start(s32[32,1]{0,1:T(1,128)} %param.10) | copy-start | bytes 388
  18.6 30.7 %all-to-all-start.7 = ((bf16[4,256,1024]{2,1,0:T(8,128)(2,1)}), bf16[4,256,1024]{2,1,0:T(8,128)(2,1)S(1)}, u32[]{:S(2)}, u32[]{:S(2)}) async-start(bf16[4,256,1024]{2,1,0:T(8,128)(2,1)} %broadcast_in_dim.115), calls=%async_computation.7 | async-start | bytes 4194304 | tf_op jit(solution)/shard_map/all_to_all | solution.py:366
  60.0 100.2 %all-to-all-start.3 = ((bf16[32,5,192,128]{3,2,1,0:T(8,128)(2,1)}), bf16[32,5,192,128]{3,2,1,0:T(8,128)(2,1)}, u32[]{:S(2)}, u32[]{:S(2)}) async-start(bf16[32,5,192,128]{3,2,1,0:T(8,128)(2,1)} %pack5.1), calls=%async_computation.3 | async-start | bytes 15728640 | tf_op jit(solution)/shard_map/cond/branch_1_fun/all_to_all | solution.py:356
  395.0 1.3 copy-start

commit v2 on v1

v2 whole, which is shorter than its diff:
```python
import functools

import jax
import jax.numpy as jnp
from jax import lax
from jax.experimental import pallas as pl
from jax.experimental.pallas import tpu as pltpu
from jax.sharding import PartitionSpec as P


BLOCK = 128
HEAD = 64
MAIN = 5
FIRST = 2
FULL = 8
TILE = 4
NT = (((1,), (1,)), ((), ()))


def tables(cluster):
    n = lax.axis_size("seq")
    me = lax.axis_index("seq")
    blocks = cluster.shape[0]
    mine = cluster.reshape(blocks)
    everyone = lax.all_to_all(
        jnp.broadcast_to(mine[None, :], (n, blocks)), "seq", split_axis=0, concat_axis=0, tiled=True
    )
    ids = jnp.arange(n, dtype=jnp.int32)
    heads = jnp.arange(4, dtype=jnp.int32)
    counts = jnp.sum((everyone[:, :, None] == ids).astype(jnp.int32), axis=1)
    weight = jnp.max(counts, axis=0)
    before = ids[None, :] < ids[:, None]
    rank2 = jnp.sum((before & (weight == 2)[None, :]).astype(jnp.int32), axis=1)
    rank1 = jnp.sum((before & (weight == 1)[None, :]).astype(jnp.int32), axis=1)
    twos = 4 * jnp.sum((weight == 2).astype(jnp.int32))
    full, rem = twos // n, twos % n
    light = n - rem
    heavy = jnp.maximum(rem, 1)
    k2 = rank2[:, None] * 4 + heads
    k = rank1[:, None] * 4 + heads
    a = jnp.maximum(MAIN - 2 * full, 0) * light
    b = jnp.maximum(MAIN - 2 - 2 * full, 0) * rem
    c0 = jnp.maximum(MAIN, 2 * full)
    c = (FULL - c0) * light
    kb, kc = k - a, k - a - b
    kd = kc - c
    owner1 = jnp.where(
        k < a, rem + k % light, jnp.where(kb < b, kb % heavy, jnp.where(kc < c, rem + kc % light, kd % heavy))
    )
    slot1 = jnp.where(
        k < a,
        2 * full + k // light,
        jnp.where(
            kb < b,
            2 * full + 2 + kb // heavy,
            jnp.where(kc < c, c0 + kc // light, jnp.maximum(MAIN, 2 * full + 2) + kd // heavy),
        ),
    )
    two = (weight == 2)[:, None]
    used = (weight > 0)[:, None]
    owner = jnp.where(two, k2 % n, owner1)
    slot = jnp.where(two, 2 * (k2 // n), slot1)
    fits = jnp.all(~used | (slot + weight[:, None] <= MAIN))
    hit = mine[:, None] == ids[None, :]
    earlier = jnp.arange(blocks)[None, :] < jnp.arange(blocks)[:, None]
    second = jnp.sum((earlier & (mine[None, :] == mine[:, None])).astype(jnp.int32), axis=1)
    target = jnp.sum(jnp.where(hit[:, :, None], (owner * FULL + slot)[None], 0), axis=1) + second[:, None]
    slots = jnp.arange(FULL, dtype=jnp.int32)
    held = (used & (owner == me))[None] & (slot[None] == slots[:, None, None])
    unit = jnp.sum(jnp.where(held, weight[None, :, None], 0), axis=(1, 2))
    count = jnp.sum(jnp.where(jnp.any(held, axis=2)[:, None, :], counts[None], 0), axis=2)
    return fits, target.reshape(blocks * 4), unit, count.reshape(FULL * n)


PACK = 4


def pack_kernel(target, q_ref, k_ref, v_ref, one_ref, two_ref, stage, eye, sems):
    step = pl.program_id(0)
    par = lax.rem(step, 2)

    @pl.when(step == 0)
    def _():
        r = lax.broadcasted_iota(jnp.int32, (256, 256), 0)
        c = lax.broadcasted_iota(jnp.int32, (256, 256), 1)
        eye[...] = jnp.where(r == c, 1.0, 0.0).astype(jnp.bfloat16)

    def send(p, i):
        t = target[step * (PACK * 4) + i]
        owner, slot = lax.div(t, FULL), lax.rem(t, FULL)

        @pl.when(slot < FIRST)
        def _():
            pltpu.make_async_copy(stage.at[p, i], one_ref.at[owner, slot], sems.at[p, i]).start()

        @pl.when(slot >= FIRST)
        def _():
            pltpu.make_async_copy(stage.at[p, i], two_ref.at[owner, slot - FIRST], sems.at[p, i]).start()

    def wait(p, i):
        pltpu.make_async_copy(stage.at[p, i], one_ref.at[0, 0], sems.at[p, i]).wait()

    @pl.when(step >= 2)
    def _():
        for i in range(PACK * 4):
            wait(par, i)

    lane = lax.broadcasted_iota(jnp.int32, (BLOCK, 128), 1)
    for t in range(PACK):
        rows = slice(t * BLOCK, (t + 1) * BLOCK)
        vt = lax.dot_general(eye[...], v_ref[rows, :], NT, preferred_element_type=jnp.float32)
        vt = vt.astype(jnp.bfloat16)
        for pair in range(2):
            cols = slice(pair * 128, (pair + 1) * 128)
            q = q_ref[rows, cols].astype(jnp.float32)
            k = k_ref[rows, cols].astype(jnp.float32)
            even = jnp.where(lane < HEAD, q, pltpu.roll(k, HEAD, 1))
            odd = jnp.where(lane < HEAD, pltpu.roll(q, HEAD, 1), k)
            stage[par, t * 4 + pair * 2, 0:BLOCK, :] = even.astype(jnp.bfloat16)
            stage[par, t * 4 + pair * 2 + 1, 0:BLOCK, :] = odd.astype(jnp.bfloat16)
        for h in range(4):
            stage[par, t * 4 + h, BLOCK : BLOCK + HEAD, :] = vt[h * HEAD : (h + 1) * HEAD]
    for i in range(PACK * 4):
        send(par, i)

    @pl.when(step == pl.num_programs(0) - 1)
    def _():
        for i in range(PACK * 4):
            wait(1 - par, i)
        for i in range(PACK * 4):
            wait(par, i)


def pack(target, queries, keys, values, n, depth):
    rows, width = queries.shape
    tile = pl.BlockSpec((PACK * BLOCK, width), lambda i, *_: (i, 0))
    return pl.pallas_call(
        pack_kernel,
        out_shape=[
            jax.ShapeDtypeStruct((n, d, BLOCK + HEAD, 128), jnp.bfloat16) for d in (FIRST, depth - FIRST)
        ],
        grid_spec=pltpu.PrefetchScalarGridSpec(
            num_scalar_prefetch=1,
            grid=(rows // (PACK * BLOCK),),
            in_specs=[tile, tile, tile],
            out_specs=[pl.BlockSpec(memory_space=pl.ANY)] * 2,
            scratch_shapes=[
                pltpu.VMEM((2, PACK * 4, BLOCK + HEAD, 128), jnp.bfloat16),
                pltpu.VMEM((256, 256), jnp.bfloat16),
                pltpu.SemaphoreType.DMA((2, PACK * 4)),
            ],
        ),
    )(target, queries, keys, values)


def attend_kernel(
    depth, offset, n, unit, count, recv, _, out, kq, qz, vt, score0, score1, top, acc, flat, where_from, steps, in_sems, out_sem
):
    tq = TILE * BLOCK
    spare = acc.shape[0] - 1

    def fetch(pos, s, j, u):
        at = pl.multiple_of(pos * BLOCK, BLOCK)
        return (
            pltpu.make_async_copy(
                recv.at[s, j, pl.ds(0, BLOCK), :], kq.at[pl.ds(at, BLOCK), :], in_sems.at[u, 0]
            ),
            pltpu.make_async_copy(
                recv.at[s, j, pl.ds(BLOCK, HEAD), :],
                vt.at[pl.ds(0, HEAD), pl.ds(at, BLOCK)],
                in_sems.at[u, 1],
            ),
        )

    def fetch_unit(u, carry):
        base, listed, total = carry
        w = unit[u]

        def source(s, pos):
            here = jnp.where(w > 0, count[u * n + s], 0)
            for r in range(2):

                @pl.when(here > r)
                def _():
                    where_from[pos + r] = s * depth + u + r
                    for c in fetch(pos + r, s, u + r, u):
                        c.start()

            return pos + here

        end = lax.fori_loop(0, n, source, base)
        stop = lax.div(end + TILE - 1, TILE) * TILE

        def blank(pos, c):
            at = pl.multiple_of(pos * BLOCK, BLOCK)
            vt[0:HEAD, pl.ds(at, BLOCK)] = jnp.zeros((HEAD, BLOCK), jnp.bfloat16)
            where_from[pos] = -1
            return c

        lax.fori_loop(end, stop, blank, 0)
        first, last = lax.div(base, TILE), lax.div(stop, TILE)

        def list_tile(q, at):
            def one(k, at):
                steps[at] = q * 256 + k
                return at + 1

            return lax.fori_loop(first, q, one, at)

        return stop, lax.fori_loop(first, last, list_tile, listed), total + end - base

    stop, listed, total = lax.fori_loop(0, depth, fetch_unit, (0, 0, 0))
    tiles = lax.div(stop, TILE)
    for extra in range(3):
        steps[listed + extra] = spare * 256 + spare
    ones = lax.broadcasted_iota(jnp.int32, (16, vt.shape[1]), 0)
    vt[HEAD : HEAD + 16, :] = jnp.where(ones == 0, 1.0, 0.0).astype(jnp.bfloat16)

    def arrive(u, c):
        def one(s, c):
            here = jnp.where(unit[u] > 0, count[u * n + s], 0)
            for r in range(2):

                @pl.when(here > r)
                def _():
                    for cp in fetch(0, 0, 0, u):
                        cp.wait()

            return c

        return lax.fori_loop(0, n, one, c)

    lax.fori_loop(0, depth, arrive, 0)

    lane = lax.broadcasted_iota(jnp.int32, (tq, 128), 1)

    def rows(tile):
        return pl.ds(pl.multiple_of(tile * tq, tq), tq)

    def score_own(tile, score):
        x = kq[rows(tile), :].astype(jnp.float32)
        q = jnp.where(lane >= HEAD, pltpu.roll(x, HEAD, 1) * 0.125, 0.0).astype(jnp.bfloat16)
        qz[rows(tile), :] = q
        s = lax.dot_general(kq[rows(tile), :], q, NT, preferred_element_type=jnp.float32)
        krow = lax.broadcasted_iota(jnp.int32, (tq, tq), 0)
        qcol = lax.broadcasted_iota(jnp.int32, (tq, tq), 1)
        s = jnp.where(krow <= qcol, s, -1e30)
        score[...] = s
        newer = jnp.max(s, axis=0, keepdims=True)
        top[tile] = newer
        return newer

    def weigh_own(tile, score, newer):
        weights = jnp.exp(score[...] - newer).astype(jnp.bfloat16)
        acc[tile] = jnp.dot(vt[:, rows(tile)], weights, preferred_element_type=jnp.float32)

    def own(i, newer):
        t = 2 * i
        following = jnp.minimum(t + 1, spare)
        later = score_own(following, score1)
        weigh_own(t, score0, newer)
        after = jnp.minimum(t + 2, spare)
        newer = score_own(after, score0)
        weigh_own(following, score1, later)
        return newer

    lax.fori_loop(0, lax.div(tiles + 1, 2), own, score_own(0, score0))

    def score_pair(at, score):
        q, k = lax.div(steps[at], 256), lax.rem(steps[at], 256)
        s = lax.dot_general(kq[rows(k), :], qz[rows(q), :], NT, preferred_element_type=jnp.float32)
        score[...] = s
        old = top[q]
        newer = jnp.maximum(old, jnp.max(s, axis=0, keepdims=True))
        top[q] = newer
        return newer, jnp.exp(old - newer)

    def weigh_pair(at, score, state):
        q, k = lax.div(steps[at], 256), lax.rem(steps[at], 256)
        weights = jnp.exp(score[...] - state[0]).astype(jnp.bfloat16)
        part = jnp.dot(vt[:, rows(k)], weights, preferred_element_type=jnp.float32)
        acc[q] = acc[q] * state[1] + part

    def pair(i, state):
        t = 2 * i
        later = score_pair(t + 1, score1)
        weigh_pair(t, score0, state)
        state = score_pair(t + 2, score0)
        weigh_pair(t + 1, score1, later)
        return state

    lax.fori_loop(0, lax.div(listed + 1, 2), pair, score_pair(0, score0))

    er = lax.broadcasted_iota(jnp.int32, (BLOCK, BLOCK), 0)
    ec = lax.broadcasted_iota(jnp.int32, (BLOCK, BLOCK), 1)
    eye = jnp.where(er == ec, 1.0, 0.0).astype(jnp.bfloat16)
    low = ec < HEAD

    def put(pos):
        f = where_from[pos]
        return pltpu.make_async_copy(
            flat.at[pos], out.at[pl.ds(lax.div(f, depth) * 4, 4), lax.rem(f, depth) + offset], out_sem
        )

    def finish(tile, c):
        o = (acc[tile, 0:HEAD] / acc[tile, HEAD : HEAD + 1]).astype(jnp.bfloat16)
        for t in range(TILE):
            pos = tile * TILE + t
            piece = o[:, t * BLOCK : (t + 1) * BLOCK]
            both = jnp.concatenate([piece, piece], axis=0)
            nat = lax.dot_general(eye, both, NT, preferred_element_type=jnp.float32)
            packed = jnp.where(low[0:HEAD], nat[0:HEAD], nat[HEAD:BLOCK]).astype(jnp.bfloat16)
            flat[pos] = packed.reshape(4, 16, 128)

        for t in range(TILE):
            pos = tile * TILE + t

            @pl.when(where_from[pos] >= 0)
            def _():
                put(pos).start()

        return c

    lax.fori_loop(0, tiles, finish, 0)

    def left(i, c):
        put(0).wait()
        return c

    lax.fori_loop(0, total, left, 0)


def attend(unit, count, recv, offset, total, earlier=None):
    n, depth = recv.shape[:2]
    tiles = -(-(depth * n + depth * (TILE - 1)) // TILE)
    pairs = depth // 2 * 120 + depth % 2 * 28
    tq = TILE * BLOCK
    smem = pl.BlockSpec(memory_space=pltpu.SMEM)
    hbm = pl.BlockSpec(memory_space=pl.ANY)
    first = earlier is None
    return pl.pallas_call(
        functools.partial(attend_kernel, depth, offset, n),
        out_shape=jax.ShapeDtypeStruct((n * 4, total, 16, 128), jnp.bfloat16),
        in_specs=[smem, smem, hbm, smem if first else hbm],
        input_output_aliases={} if first else {3: 0},
        out_specs=pl.BlockSpec(memory_space=pl.ANY),
        scratch_shapes=[
            pltpu.VMEM(((tiles + 1) * tq, 128), jnp.bfloat16),
            pltpu.VMEM(((tiles + 1) * tq, 128), jnp.bfloat16),
            pltpu.VMEM((HEAD + 16, (tiles + 1) * tq), jnp.bfloat16),
            pltpu.VMEM((tq, tq), jnp.float32),
            pltpu.VMEM((tq, tq), jnp.float32),
            pltpu.VMEM((tiles + 1, 1, tq), jnp.float32),
            pltpu.VMEM((tiles + 1, HEAD + 16, tq), jnp.float32),
            pltpu.VMEM((tiles * TILE, 4, 16, 128), jnp.bfloat16),
            pltpu.SMEM((tiles * TILE + 4,), jnp.int32),
            pltpu.SMEM((pairs + 4,), jnp.int32),
            pltpu.SemaphoreType.DMA((depth, 2)),
            pltpu.SemaphoreType.DMA,
        ],
        compiler_params=pltpu.CompilerParams(vmem_limit_bytes=60 * 2**20),
        cost_estimate=pl.CostEstimate(
            flops=depth * 10**10, bytes_accessed=depth * 4 * 10**7, transcendentals=depth * 3 * 10**7
        ),
    )(unit, count, recv, unit if first else earlier)


PROJ = 8


def project_kernel(target, got, w_ref, out_ref, att):
    step = pl.program_id(0)
    lane = lax.broadcasted_iota(jnp.int32, (16, 128), 1)

    def piece(entry, z):
        owner, slot = lax.div(entry, FULL) * 4 + z, lax.rem(entry, FULL)
        return got[owner, slot].astype(jnp.float32)

    for t in range(PROJ):
        for pair in range(2):
            at = (step * PROJ + t) * 4 + pair * 2
            ea, eb = target[at], target[at + 1]
            for z in range(4):
                even, odd = piece(ea, z), piece(eb, z)
                cols = slice(z * 256 + pair * 128, z * 256 + pair * 128 + 128)
                lo = jnp.where(lane < HEAD, even, pltpu.roll(odd, HEAD, 1))
                hi = jnp.where(lane < HEAD, pltpu.roll(even, HEAD, 1), odd)
                att[t * 32 : t * 32 + 16, cols] = lo.astype(jnp.bfloat16)
                att[t * 32 + 16 : t * 32 + 32, cols] = hi.astype(jnp.bfloat16)
    mixed = jnp.zeros((PROJ * 32, 1024), jnp.float32)
    for z in range(4):
        mixed += jnp.dot(att[:, z * 256 : (z + 1) * 256], w_ref[z], preferred_element_type=jnp.float32)
    mixed = mixed.astype(jnp.bfloat16)
    for z in range(4):
        out_ref[z] = mixed[:, z * 256 : (z + 1) * 256].reshape(PROJ, 2, 16, 256)


def project(target, got, w_full, blocks):
    return pl.pallas_call(
        project_kernel,
        out_shape=jax.ShapeDtypeStruct((4, blocks, 2, 16, 256), jnp.bfloat16),
        grid_spec=pltpu.PrefetchScalarGridSpec(
            num_scalar_prefetch=1,
            grid=(blocks // PROJ,),
            in_specs=[
                pl.BlockSpec(got.shape, lambda i, *_: (0, 0, 0, 0)),
                pl.BlockSpec(w_full.shape, lambda i, *_: (0, 0, 0)),
            ],
            out_specs=pl.BlockSpec((4, PROJ, 2, 16, 256), lambda i, *_: (0, i, 0, 0, 0)),
            scratch_shapes=[pltpu.VMEM((PROJ * 32, 1024), jnp.bfloat16)],
        ),
    )(target, got, w_full)


def route(depth, *args):
    return steps(depth, *args)


def steps(depth, target, unit, count, queries, keys, values, w_out):
    n = lax.axis_size("seq")
    blocks = queries.shape[0] // BLOCK

    def exchange(x, axes):
        return lax.all_to_all(x, axes, split_axis=0, concat_axis=0, tiled=True)

    one, two = pack(target, queries, keys, values, n, depth)
    one = exchange(one, "seq")
    one, two = lax.optimization_barrier((one, two))
    two = exchange(two, "seq")
    answers = attend(unit[:FIRST], count[: FIRST * n], one, 0, depth)
    two, w_out = lax.optimization_barrier((two, w_out))
    w_full = exchange(jnp.broadcast_to(w_out[None], (4,) + w_out.shape), "head")
    answers = attend(unit[FIRST:depth], count[FIRST * n : depth * n], two, FIRST, depth, answers)
    got = exchange(answers, ("seq", "head"))
    mixed = project(target, got, w_full, blocks)
    back = exchange(mixed, "head")
    return back.transpose(1, 2, 0, 3, 4).reshape(queries.shape)


def body(queries, keys, values, cluster, w_out):
    fits, target, unit, count = tables(cluster)
    return lax.cond(
        fits,
        functools.partial(route, MAIN),
        functools.partial(route, FULL),
        target,
        unit,
        count,
        queries,
        keys,
        values,
        w_out,
    )


def solution(mesh):
    placed = (P("seq", "head"), P("seq", "head"), P("seq", "head"), P("seq", None), P("head", None))
    return jax.shard_map(
        body, mesh=mesh, in_specs=placed, out_specs=P("seq", "head"), check_vma=False
    )
```

time: 397 us -> 272 us (0.69)
  waiting for transfers between devices: 114 us -> 6.09 us
  Pallas kernels: 168 us -> 108 us
  blocking collectives: 91.2 us -> 125 us
  starting transfers between devices: 11.4 us -> 18.5 us
    all_to_all x2 -> x3, waiting for transfers between devices: 114 us -> 6.09 us  [the longest x1 6.09 us: tables(): lax.all_to_all(jnp.broadcast_to(mine[None, :], (n, blocks)), 'seq', split...]
    pallas_call x2 -> x3, Pallas kernels: 161 us -> 101 us  [the longest x2 91.6 us: attend(): pl.pallas_call(functools.partial(attend_kernel, depth, offset, n), out_sh...]
    all_to_all x3, blocking collectives: 91.2 us -> 125 us  [exchange(): return lax.all_to_all(x, axes, split_axis=0, concat_axis=0, tiled=True)]
    all_to_all x2 -> x3, starting transfers between devices: 11.4 us -> 18.5 us  [the longest x2 9.88 us: exchange(): return lax.all_to_all(x, axes, split_axis=0, concat_axis=0, tiled=True)]
  transfers between devices with their start and end apart: 2 -> 3, of which waited for: 2 -> 1; matrix products, arithmetic and copies ran while one was open for 1% -> 1% of each run, Pallas kernels for 0% -> 34%
where the time goes in v2:
time: 272 us
  blocking collectives  125 us (46%)
  Pallas kernels  108 us (40%)
  starting transfers between devices  18.5 us (7%)
  local copies, waits for them, and re-layouts  7.82 us (3%)
  waiting for transfers between devices  6.09 us (2%)
  other arithmetic  3.66 us (1%)
    all_to_all x3, blocking collectives, exchange(): return lax.all_to_all(x, axes, split_axis=0, concat_axis=0, tiled=True)  125 us
    pallas_call x2, Pallas kernels, attend(): pl.pallas_call(functools.partial(attend_kernel, depth, offset, n), out_sh...  91.6 us
    all_to_all x2, starting transfers between devices, exchange(): return lax.all_to_all(x, axes, split_axis=0, concat_axis=0, tiled=True)  9.88 us
    pallas_call x1, Pallas kernels, pack(): pl.pallas_call(pack_kernel, out_shape=[jax.ShapeDtypeStruct((n, d, BLOCK...  9.4 us
    all_to_all x1, starting transfers between devices, tables(): lax.all_to_all(jnp.broadcast_to(mine[None, :], (n, blocks)), 'seq', split...  8.58 us
    pallas_call x1, Pallas kernels, project(): pl.pallas_call(project_kernel, out_shape=jax.ShapeDtypeStruct((4, blocks,...  7.44 us
    all_to_all x1, waiting for transfers between devices, tables(): lax.all_to_all(jnp.broadcast_to(mine[None, :], (n, blocks)), 'seq', split...  6.09 us
  transfers between devices with their start and end apart: 3, of which 1 were waited for; matrix products, arithmetic and copies ran while one was open for 1% of the time, Pallas kernels for 34%

profile of v2, /device:TPU:1, one launch (start us, length us, event | category | flops | bytes accessed | tf_op | source)
XLA Modules:
  0.0 271.5 jit_solution(5708817817310258006)
XLA Ops:
  0.0 1.3 broadcast_in_dim.78
  1.3 8.6 %all-to-all-start.10 = ((s32[32,1,32]{2,1,0:T(1,128)}), s32[32,1,32]{2,1,0:T(1,128)S(1)}, u32[]{:S(2)}, u32[]{:S(2)}) async-start(s32[32,1,32]{2,1,0:T(1,128)} %broadcast_in_dim.78), calls=%async_computation.10 | async-start | bytes 32768 | tf_op jit(solution)/shard_map/all_to_all | solution.py:25
  9.9 0.8 fusion.3
  10.7 6.1 %all-to-all-done.10 = s32[32,1,32]{2,1,0:T(1,128)S(1)} async-done(((s32[32,1,32]{2,1,0:T(1,128)}), s32[32,1,32]{2,1,0:T(1,128)S(1)}, u32[]{:S(2)}, u32[]{:S(2)}) %all-to-all-start.10) | async-done | bytes 4128 | tf_op jit(solution)/shard_map/all_to_all | solution.py:25
  16.7 0.2 convert_reduce_fusion
  17.0 0.6 convert_reduce_fusion.3
  18.4 0.1 convert_reduce_fusion.1
  18.5 0.9 fusion.40
  20.0 0.2 fusion.6
  20.2 0.7 eq.112
  21.0 249.2 %conditional.1 = (bf16[4096,256]{1,0:T(8,128)(2,1)S(1)}) conditional(s32[]{:T(128)} %convert_element_type.22, (pred[32]{0:T(512)(128)(4,1)S(1)}, s32[32,4]{0,1:T(4,128)S(1)}, s32[32,32]{1,0:T(8,128)S(1)}, bf16[4096,256]{1,0:T(8,128)(2,1)}, bf16[4096,256]{1,0:T(8,128)(2,1)}, /*index=5*/bf16[4096,256]{1,0:T(8,128)(2,1)}, ...), branch_computations={%region_11.12_spmd, %region_12.13_spmd} | conditional | flops 80000032768 | bytes 390816800 | solution.py:442
  21.0 0.1 reduce_sum.87
  21.1 0.1 select_reduce_fusion.4
  21.3 0.1 copy.30
  21.4 0.7 add.288.target
  22.1 9.4 %branch_1_fun.4 = (bf16[32,2,192,128]{3,2,1,0:T(8,128)(2,1)}, bf16[32,3,192,128]{3,2,1,0:T(8,128)(2,1)}) custom-call(s32[128]{0:T(128)} %add.288.target, bf16[4096,256]{1,0:T(8,128)(2,1)} %get-tuple-element.94.q_ref, bf16[4096,256]{1,0:T(8,128)(2,1)} %get-tuple-element.96.k_ref, bf16[4096,256]{1,0:T(8,128)(2,1)} %get-tuple-element.98.v_ref), custom_call_target="tpu_custom_call" | custom-call | tf_op jit(solution)/shard_map/cond/branch_1_fun/pallas_call | solution.py:137
  31.5 44.7 %all_to_all.49.recv = bf16[32,2,192,128]{3,2,1,0:T(8,128)(2,1)} all-to-all(bf16[32,2,192,128]{3,2,1,0:T(8,128)(2,1)} %get-tuple-element.55), channel_id=1, replica_groups=mesh['seq'=32,'head'=4] {'seq'}, dimensions={0} | all-to-all | bytes 6291456 | tf_op jit(solution)/shard_map/cond/branch_1_fun/all_to_all | solution.py:424
  76.2 4.9 %all-to-all-start.6 = ((bf16[32,3,192,128]{3,2,1,0:T(8,128)(2,1)}), bf16[32,3,192,128]{3,2,1,0:T(8,128)(2,1)}, u32[]{:S(2)}, u32[]{:S(2)}) async-start(bf16[32,3,192,128]{3,2,1,0:T(8,128)(2,1)} %get-tuple-element.57), calls=%async_computation.6 | async-start | bytes 9437184 | tf_op jit(solution)/shard_map/cond/branch_1_fun/all_to_all | solution.py:424
  81.1 0.2 select_reduce_fusion.3
  81.4 0.2 select_reduce_fusion.5
  81.6 0.7 slice.20.unit
  82.3 0.6 reshape.356.count
  82.9 0.6 reshape.357.count
  83.4 56.8 %branch_1_fun.5._ = bf16[128,5,16,128]{3,2,1,0:T(8,128)(2,1)} custom-call(s32[2]{0:T(128)} %bitcast.18, s32[64]{0:T(128)} %reshape.357.count, bf16[32,2,192,128]{3,2,1,0:T(8,128)(2,1)} %all_to_all.49.recv, s32[2]{0:T(128)} %bitcast.19), custom_call_target="tpu_custom_call" | custom-call | flops 20000000000 | bytes 80000000 | tf_op jit(solution)/shard_map/cond/branch_1_fun/pallas_call | solution.py:341
  140.3 1.6 broadcast_in_dim.49
  141.9 5.0 %all-to-all-start.8 = ((bf16[4,256,1024]{2,1,0:T(8,128)(2,1)}), bf16[4,256,1024]{2,1,0:T(8,128)(2,1)S(1)}, u32[]{:S(2)}, u32[]{:S(2)}) async-start(bf16[4,256,1024]{2,1,0:T(8,128)(2,1)} %broadcast_in_dim.49), calls=%async_computation.8 | async-start | bytes 4194304 | tf_op jit(solution)/shard_map/cond/branch_1_fun/all_to_all | solution.py:424
  146.9 34.8 %branch_1_fun.6 = bf16[128,5,16,128]{3,2,1,0:T(8,128)(2,1)} custom-call(s32[3]{0:T(128)} %slice.20.unit, s32[96]{0:T(128)} %reshape.356.count, bf16[32,3,192,128]{3,2,1,0:T(8,128)(2,1)} %all-to-all-done.6.recv, bf16[128,5,16,128]{3,2,1,0:T(8,128)(2,1)} %branch_1_fun.5._), custom_call_target="tpu_custom_call", output_to_operand_aliasing={{}: (3, {})} | custom-call | flops 30000001024 | bytes 120000000 | tf_op jit(solution)/shard_map/cond/branch_1_fun/pallas_call | solution.py:341
  181.7 50.8 %all_to_all.50.got = bf16[128,5,16,128]{3,2,1,0:T(8,128)(2,1)} all-to-all(bf16[128,5,16,128]{3,2,1,0:T(8,128)(2,1)} %branch_1_fun.6), channel_id=1, replica_groups=mesh['seq'=32,'head'=4] {'seq','head'}, dimensions={0} | all-to-all | bytes 5242880 | tf_op jit(solution)/shard_map/cond/branch_1_fun/all_to_all | solution.py:424
  232.5 7.4 %branch_1_fun.7 = bf16[4,32,2,16,256]{4,3,2,1,0:T(8,128)(2,1)} custom-call(s32[128]{0:T(128)} %add.288.target, bf16[128,5,16,128]{3,2,1,0:T(8,128)(2,1)} %all_to_all.50.got, bf16[4,256,1024]{2,1,0:T(8,128)(2,1)} %copy-done), custom_call_target="tpu_custom_call" | custom-call | tf_op jit(solution)/shard_map/cond/branch_1_fun/pallas_call | solution.py:399
  240.0 29.7 %all_to_all.51 = bf16[4,32,2,16,256]{4,3,2,1,0:T(8,128)(2,1)S(1)} all-to-all(bf16[4,32,2,16,256]{4,3,2,1,0:T(8,128)(2,1)} %branch_1_fun.7), channel_id=1, replica_groups=mesh['seq'=32,'head'=4] {'head'}, dimensions={0} | all-to-all | bytes 4194304 | tf_op jit(solution)/shard_map/cond/branch_1_fun/all_to_all | solution.py:424
  269.7 0.3 copy.31
  270.2 1.3 copy-done.4
  (22 shorter events, 0.1 us)
Async XLA Ops:
  1.3 15.5 %all-to-all-start.10 = ((s32[32,1,32]{2,1,0:T(1,128)}), s32[32,1,32]{2,1,0:T(1,128)S(1)}, u32[]{:S(2)}, u32[]{:S(2)}) async-start(s32[32,1,32]{2,1,0:T(1,128)} %broadcast_in_dim.78), calls=%async_computation.10 | async-start | bytes 32768 | tf_op jit(solution)/shard_map/all_to_all | solution.py:25
  76.2 64.1 %all-to-all-start.6 = ((bf16[32,3,192,128]{3,2,1,0:T(8,128)(2,1)}), bf16[32,3,192,128]{3,2,1,0:T(8,128)(2,1)}, u32[]{:S(2)}, u32[]{:S(2)}) async-start(bf16[32,3,192,128]{3,2,1,0:T(8,128)(2,1)} %get-tuple-element.57), calls=%async_computation.6 | async-start | bytes 9437184 | tf_op jit(solution)/shard_map/cond/branch_1_fun/all_to_all | solution.py:424
  81.6 1.8 copy-start.6
  83.4 56.8 %copy-start.3 = (bf16[256,1024]{1,0:T(8,128)(2,1)S(1)}, bf16[256,1024]{1,0:T(8,128)(2,1)}, u32[]{:S(2)}) copy-start(bf16[256,1024]{1,0:T(8,128)(2,1)} %get-tuple-element.61) | copy-start | bytes 1572868 | tf_op jit(solution)/shard_map/cond
  141.9 39.9 %all-to-all-start.8 = ((bf16[4,256,1024]{2,1,0:T(8,128)(2,1)}), bf16[4,256,1024]{2,1,0:T(8,128)(2,1)S(1)}, u32[]{:S(2)}, u32[]{:S(2)}) async-start(bf16[4,256,1024]{2,1,0:T(8,128)(2,1)} %broadcast_in_dim.49), calls=%async_computation.8 | async-start | bytes 4194304 | tf_op jit(solution)/shard_map/cond/branch_1_fun/all_to_all | solution.py:424
  181.7 50.8 %copy-start = (bf16[4,256,1024]{2,1,0:T(8,128)(2,1)}, bf16[4,256,1024]{2,1,0:T(8,128)(2,1)S(1)}, u32[]{:S(2)}) copy-start(bf16[4,256,1024]{2,1,0:T(8,128)(2,1)S(1)} %all-to-all-done.8.w_ref) | copy-start | bytes 6291460 | tf_op jit(solution)/shard_map/cond
  270.2 1.3 copy-start.4

commit v3 on v2

--- a/solution.py
+++ b/solution.py
@@ -11,7 +11,7 @@
 BLOCK = 128
 HEAD = 64
 MAIN = 5
-FIRST = 2
+CUTS = (2,)
 FULL = 8
 TILE = 4
 NT = (((1,), (1,)), ((), ()))
@@ -89,13 +89,11 @@
         t = target[step * (PACK * 4) + i]
         owner, slot = lax.div(t, FULL), lax.rem(t, FULL)
 
-        @pl.when(slot < FIRST)
-        def _():
-            pltpu.make_async_copy(stage.at[p, i], one_ref.at[owner, slot], sems.at[p, i]).start()
-
-        @pl.when(slot >= FIRST)
-        def _():
-            pltpu.make_async_copy(stage.at[p, i], two_ref.at[owner, slot - FIRST], sems.at[p, i]).start()
+        for ref, low, high in zip((one_ref, two_ref), (0,) + CUTS, CUTS + (FULL,)):
+
+            @pl.when((slot >= low) & (slot < high))
+            def _():
+                pltpu.make_async_copy(stage.at[p, i], ref.at[owner, slot - low], sems.at[p, i]).start()
 
     def wait(p, i):
         pltpu.make_async_copy(stage.at[p, i], one_ref.at[0, 0], sems.at[p, i]).wait()
@@ -137,7 +135,8 @@
     return pl.pallas_call(
         pack_kernel,
         out_shape=[
-            jax.ShapeDtypeStruct((n, d, BLOCK + HEAD, 128), jnp.bfloat16) for d in (FIRST, depth - FIRST)
+            jax.ShapeDtypeStruct((n, high - low, BLOCK + HEAD, 128), jnp.bfloat16)
+            for low, high in zip((0,) + CUTS, CUTS + (depth,))
         ],
         grid_spec=pltpu.PrefetchScalarGridSpec(
             num_scalar_prefetch=1,
@@ -211,6 +210,8 @@
 
     stop, listed, total = lax.fori_loop(0, depth, fetch_unit, (0, 0, 0))
     tiles = lax.div(stop, TILE)
+    for extra in range(TILE):
+        where_from[stop + extra] = -1
     for extra in range(3):
         steps[listed + extra] = spare * 256 + spare
     ones = lax.broadcasted_iota(jnp.int32, (16, vt.shape[1]), 0)
@@ -302,7 +303,7 @@
             flat.at[pos], out.at[pl.ds(lax.div(f, depth) * 4, 4), lax.rem(f, depth) + offset], out_sem
         )
 
-    def finish(tile, c):
+    def finish(tile):
         o = (acc[tile, 0:HEAD] / acc[tile, HEAD : HEAD + 1]).astype(jnp.bfloat16)
         for t in range(TILE):
             pos = tile * TILE + t
@@ -312,8 +313,11 @@
             packed = jnp.where(low[0:HEAD], nat[0:HEAD], nat[HEAD:BLOCK]).astype(jnp.bfloat16)
             flat[pos] = packed.reshape(4, 16, 128)
 
-        for t in range(TILE):
-            pos = tile * TILE + t
+    def finish_two(i, c):
+        finish(2 * i)
+        finish(2 * i + 1)
+        for t in range(2 * TILE):
+            pos = i * 2 * TILE + t
 
             @pl.when(where_from[pos] >= 0)
             def _():
@@ -321,7 +325,7 @@
 
         return c
 
-    lax.fori_loop(0, tiles, finish, 0)
+    lax.fori_loop(0, lax.div(tiles + 1, 2), finish_two, 0)
 
     def left(i, c):
         put(0).wait()
@@ -352,8 +356,8 @@
             pltpu.VMEM((tq, tq), jnp.float32),
             pltpu.VMEM((tiles + 1, 1, tq), jnp.float32),
             pltpu.VMEM((tiles + 1, HEAD + 16, tq), jnp.float32),
-            pltpu.VMEM((tiles * TILE, 4, 16, 128), jnp.bfloat16),
-            pltpu.SMEM((tiles * TILE + 4,), jnp.int32),
+            pltpu.VMEM(((tiles + 1) * TILE, 4, 16, 128), jnp.bfloat16),
+            pltpu.SMEM(((tiles + 1) * TILE,), jnp.int32),
             pltpu.SMEM((pairs + 4,), jnp.int32),
             pltpu.SemaphoreType.DMA((depth, 2)),
             pltpu.SemaphoreType.DMA,
@@ -368,7 +372,7 @@
 PROJ = 8
 
 
-def project_kernel(target, got, w_ref, out_ref, att):
+def project_kernel(target, group, got, w0, w1, w2, w3, out_ref, att):
     step = pl.program_id(0)
     lane = lax.broadcasted_iota(jnp.int32, (16, 128), 1)
 
@@ -381,35 +385,37 @@
             at = (step * PROJ + t) * 4 + pair * 2
             ea, eb = target[at], target[at + 1]
             for z in range(4):
-                even, odd = piece(ea, z), piece(eb, z)
+                source = lax.rem(group[0] + z, 4)
+                even, odd = piece(ea, source), piece(eb, source)
                 cols = slice(z * 256 + pair * 128, z * 256 + pair * 128 + 128)
                 lo = jnp.where(lane < HEAD, even, pltpu.roll(odd, HEAD, 1))
                 hi = jnp.where(lane < HEAD, pltpu.roll(even, HEAD, 1), odd)
                 att[t * 32 : t * 32 + 16, cols] = lo.astype(jnp.bfloat16)
                 att[t * 32 + 16 : t * 32 + 32, cols] = hi.astype(jnp.bfloat16)
     mixed = jnp.zeros((PROJ * 32, 1024), jnp.float32)
-    for z in range(4):
-        mixed += jnp.dot(att[:, z * 256 : (z + 1) * 256], w_ref[z], preferred_element_type=jnp.float32)
+    for z, w in enumerate((w0, w1, w2, w3)):
+        mixed += jnp.dot(att[:, z * 256 : (z + 1) * 256], w[...], preferred_element_type=jnp.float32)
     mixed = mixed.astype(jnp.bfloat16)
     for z in range(4):
         out_ref[z] = mixed[:, z * 256 : (z + 1) * 256].reshape(PROJ, 2, 16, 256)
 
 
-def project(target, got, w_full, blocks):
+def project(target, got, weights, blocks):
+    group = lax.axis_index("head").reshape(1)
     return pl.pallas_call(
         project_kernel,
         out_shape=jax.ShapeDtypeStruct((4, blocks, 2, 16, 256), jnp.bfloat16),
         grid_spec=pltpu.PrefetchScalarGridSpec(
-            num_scalar_prefetch=1,
+            num_scalar_prefetch=2,
             grid=(blocks // PROJ,),
             in_specs=[
                 pl.BlockSpec(got.shape, lambda i, *_: (0, 0, 0, 0)),
-                pl.BlockSpec(w_full.shape, lambda i, *_: (0, 0, 0)),
-            ],
+            ]
+            + [pl.BlockSpec(w.shape, lambda i, *_: (0, 0)) for w in weights],
             out_specs=pl.BlockSpec((4, PROJ, 2, 16, 256), lambda i, *_: (0, i, 0, 0, 0)),
             scratch_shapes=[pltpu.VMEM((PROJ * 32, 1024), jnp.bfloat16)],
         ),
-    )(target, got, w_full)
+    )(target, group, got, *weights)
 
 
 def route(depth, *args):
@@ -427,12 +433,14 @@
     one = exchange(one, "seq")
     one, two = lax.optimization_barrier((one, two))
     two = exchange(two, "seq")
-    answers = attend(unit[:FIRST], count[: FIRST * n], one, 0, depth)
-    two, w_out = lax.optimization_barrier((two, w_out))
-    w_full = exchange(jnp.broadcast_to(w_out[None], (4,) + w_out.shape), "head")
-    answers = attend(unit[FIRST:depth], count[FIRST * n : depth * n], two, FIRST, depth, answers)
+    weights = [w_out]
+    for r in (1, 2, 3):
+        weights.append(lax.ppermute(w_out, "head", [((z + r) % 4, z) for z in range(4)]))
+    a = CUTS[0]
+    answers = attend(unit[:a], count[: a * n], one, 0, depth)
+    answers = attend(unit[a:depth], count[a * n : depth * n], two, a, depth, answers)
     got = exchange(answers, ("seq", "head"))
-    mixed = project(target, got, w_full, blocks)
+    mixed = project(target, got, weights, blocks)
     back = exchange(mixed, "head")
     return back.transpose(1, 2, 0, 3, 4).reshape(queries.shape)
 

time: 272 us -> 284 us (1.044)
  blocking collectives: 125 us -> 74.3 us
  waiting for transfers between devices: 6.09 us -> 56.5 us
  starting transfers between devices: 18.5 us -> 33.4 us
    all_to_all x3 -> x2, blocking collectives: 125 us -> 74.3 us  [exchange(): return lax.all_to_all(x, axes, split_axis=0, concat_axis=0, tiled=True)]
    ppermute x0 -> x3, waiting for transfers between devices: none -> 50.4 us  [steps(): lax.ppermute(w_out, 'head', [((z + r) % 4, z) for z in range(4)])]
    all_to_all x2, starting transfers between devices: 9.88 us -> 20.6 us  [exchange(): return lax.all_to_all(x, axes, split_axis=0, concat_axis=0, tiled=True)]
    ppermute x0 -> x3, starting transfers between devices: none -> 4.19 us  [steps(): lax.ppermute(w_out, 'head', [((z + r) % 4, z) for z in range(4)])]
  transfers between devices with their start and end apart: 3 -> 6, of which waited for: 1 -> 4; matrix products, arithmetic and copies ran while one was open for 1% -> 1% of each run, Pallas kernels for 34% -> 20%
where the time goes in v3:
time: 284 us
  Pallas kernels  106 us (37%)
  blocking collectives  74.3 us (26%)
  waiting for transfers between devices  56.5 us (20%)
  starting transfers between devices  33.4 us (12%)
  local copies, waits for them, and re-layouts  7.71 us (3%)
  other arithmetic  3.66 us (1%)
    pallas_call x2, Pallas kernels, attend(): pl.pallas_call(functools.partial(attend_kernel, depth, offset, n), out_sh...  89.5 us
    all_to_all x2, blocking collectives, exchange(): return lax.all_to_all(x, axes, split_axis=0, concat_axis=0, tiled=True)  74.3 us
    ppermute x3, waiting for transfers between devices, steps(): lax.ppermute(w_out, 'head', [((z + r) % 4, z) for z in range(4)])  50.4 us
    all_to_all x2, starting transfers between devices, exchange(): return lax.all_to_all(x, axes, split_axis=0, concat_axis=0, tiled=True)  20.6 us
    pallas_call x1, Pallas kernels, pack(): pl.pallas_call(pack_kernel, out_shape=[jax.ShapeDtypeStruct((n, high - lo...  9.36 us
    all_to_all x1, starting transfers between devices, tables(): lax.all_to_all(jnp.broadcast_to(mine[None, :], (n, blocks)), 'seq', split...  8.58 us
    pallas_call x1, Pallas kernels, project(): pl.pallas_call(project_kernel, out_shape=jax.ShapeDtypeStruct((4, blocks,...  7.41 us
    all_to_all x1, waiting for transfers between devices, tables(): lax.all_to_all(jnp.broadcast_to(mine[None, :], (n, blocks)), 'seq', split...  6.09 us
  transfers between devices with their start and end apart: 6, of which 4 were waited for; matrix products, arithmetic and copies ran while one was open for 1% of the time, Pallas kernels for 20%

profile of v3, /device:TPU:1, one launch (start us, length us, event | category | flops | bytes accessed | tf_op | source)
XLA Modules:
  0.0 283.6 jit_solution(17172578568106455626)
XLA Ops:
  0.0 1.3 broadcast_in_dim.98
  1.3 8.6 %all-to-all-start.8 = ((s32[32,1,32]{2,1,0:T(1,128)}), s32[32,1,32]{2,1,0:T(1,128)S(1)}, u32[]{:S(2)}, u32[]{:S(2)}) async-start(s32[32,1,32]{2,1,0:T(1,128)} %broadcast_in_dim.98), calls=%async_computation.8 | async-start | bytes 32768 | tf_op jit(solution)/shard_map/all_to_all | solution.py:25
  9.9 0.8 fusion.3
  10.7 6.1 %all-to-all-done.8 = s32[32,1,32]{2,1,0:T(1,128)S(1)} async-done(((s32[32,1,32]{2,1,0:T(1,128)}), s32[32,1,32]{2,1,0:T(1,128)S(1)}, u32[]{:S(2)}, u32[]{:S(2)}) %all-to-all-start.8) | async-done | bytes 4128 | tf_op jit(solution)/shard_map/all_to_all | solution.py:25
  16.7 0.2 convert_reduce_fusion
  17.0 0.6 convert_reduce_fusion.3
  18.5 0.9 fusion.40
  20.0 0.2 fusion.6
  20.2 0.7 eq.112
  21.0 261.3 %conditional.1 = (bf16[4096,256]{1,0:T(8,128)(2,1)S(1)}) conditional(s32[]{:T(128)} %convert_element_type.22, (pred[32]{0:T(512)(128)(4,1)S(1)}, s32[32,4]{0,1:T(4,128)S(1)}, s32[32,32]{1,0:T(8,128)S(1)}, bf16[4096,256]{1,0:T(8,128)(2,1)}, bf16[4096,256]{1,0:T(8,128)(2,1)}, /*index=5*/bf16[4096,256]{1,0:T(8,128)(2,1)}, ...), branch_computations={%region_11.12_spmd, %region_12.13_spmd} | conditional | flops 80000032768 | bytes 390292704 | solution.py:450
  21.4 0.7 add.288.target
  22.0 9.4 %branch_1_fun.4 = (bf16[32,2,192,128]{3,2,1,0:T(8,128)(2,1)}, bf16[32,3,192,128]{3,2,1,0:T(8,128)(2,1)}) custom-call(s32[128]{0:T(128)} %add.288.target, bf16[4096,256]{1,0:T(8,128)(2,1)} %get-tuple-element.90.q_ref, bf16[4096,256]{1,0:T(8,128)(2,1)} %get-tuple-element.92.k_ref, bf16[4096,256]{1,0:T(8,128)(2,1)} %get-tuple-element.94.v_ref), custom_call_target="tpu_custom_call" | custom-call | tf_op jit(solution)/shard_map/cond/branch_1_fun/pallas_call | solution.py:135
  31.4 44.7 %all_to_all.40.recv = bf16[32,2,192,128]{3,2,1,0:T(8,128)(2,1)} all-to-all(bf16[32,2,192,128]{3,2,1,0:T(8,128)(2,1)} %get-tuple-element.53), channel_id=1, replica_groups=mesh['seq'=32,'head'=4] {'seq'}, dimensions={0} | all-to-all | bytes 6291456 | tf_op jit(solution)/shard_map/cond/branch_1_fun/all_to_all | solution.py:430
  76.2 5.0 %all-to-all-start.5 = ((bf16[32,3,192,128]{3,2,1,0:T(8,128)(2,1)}), bf16[32,3,192,128]{3,2,1,0:T(8,128)(2,1)}, u32[]{:S(2)}, u32[]{:S(2)}) async-start(bf16[32,3,192,128]{3,2,1,0:T(8,128)(2,1)} %get-tuple-element.55), calls=%async_computation.5 | async-start | bytes 9437184 | tf_op jit(solution)/shard_map/cond/branch_1_fun/all_to_all | solution.py:430
  81.3 0.2 select_reduce_fusion.3
  81.5 0.2 select_reduce_fusion.5
  81.7 0.6 slice.20.unit
  82.3 0.7 reshape.360.count
  83.0 0.6 reshape.361.count
  83.6 55.7 %branch_1_fun.5._ = bf16[128,5,16,128]{3,2,1,0:T(8,128)(2,1)} custom-call(s32[2]{0:T(128)} %bitcast.20, s32[64]{0:T(128)} %reshape.361.count, bf16[32,2,192,128]{3,2,1,0:T(8,128)(2,1)} %all_to_all.40.recv, s32[2]{0:T(128)} %bitcast.21), custom_call_target="tpu_custom_call" | custom-call | flops 20000000000 | bytes 80000000 | tf_op jit(solution)/shard_map/cond/branch_1_fun/pallas_call | solution.py:345
  139.3 33.8 %branch_1_fun.6 = bf16[128,5,16,128]{3,2,1,0:T(8,128)(2,1)} custom-call(s32[3]{0:T(128)} %slice.20.unit, s32[96]{0:T(128)} %reshape.360.count, bf16[32,3,192,128]{3,2,1,0:T(8,128)(2,1)} %all-to-all-done.5.recv, bf16[128,5,16,128]{3,2,1,0:T(8,128)(2,1)} %branch_1_fun.5._), custom_call_target="tpu_custom_call", output_to_operand_aliasing={{}: (3, {})} | custom-call | flops 30000001024 | bytes 120000000 | tf_op jit(solution)/shard_map/cond/branch_1_fun/pallas_call | solution.py:345
  173.1 15.6 %all-to-all-start.6 = ((bf16[128,5,16,128]{3,2,1,0:T(8,128)(2,1)}), bf16[128,5,16,128]{3,2,1,0:T(8,128)(2,1)S(1)}, u32[]{:S(2)}, u32[]{:S(2)}) async-start(bf16[128,5,16,128]{3,2,1,0:T(8,128)(2,1)} %branch_1_fun.6), calls=%async_computation.6 | async-start | bytes 5242880 | tf_op jit(solution)/shard_map/cond/branch_1_fun/all_to_all | solution.py:430
  188.7 3.3 %collective-permute-start.3 = (bf16[256,1024]{1,0:T(8,128)(2,1)S(1)}, bf16[256,1024]{1,0:T(8,128)(2,1)}, u32[]{:S(2)}, u32[]{:S(2)}) collective-permute-start(bf16[256,1024]{1,0:T(8,128)(2,1)S(1)} %copy-done.2), channel_id=1, source_target_pairs={{1,0},{2,1},{3,2},{0,3},{5,4},{6,5},{7,6},{4,7},{9,8},{10,9},{11,1... | collective-permute-start | bytes 1572872 | tf_op jit(solution)/shard_map/cond/branch_1_fun/ppermute | solution.py:438
  192.1 0.8 collective-permute-start.5
  192.9 37.1 %collective-permute-done.3.w1 = bf16[256,1024]{1,0:T(8,128)(2,1)} collective-permute-done((bf16[256,1024]{1,0:T(8,128)(2,1)S(1)}, bf16[256,1024]{1,0:T(8,128)(2,1)}, u32[]{:S(2)}, u32[]{:S(2)}) %collective-permute-start.3) | collective-permute-done | bytes 524320 | tf_op jit(solution)/shard_map/cond/branch_1_fun/ppermute | solution.py:438
  230.0 2.7 collective-permute-done.4.w2
  232.7 10.6 %collective-permute-done.5.w3 = bf16[256,1024]{1,0:T(8,128)(2,1)} collective-permute-done((bf16[256,1024]{1,0:T(8,128)(2,1)S(1)}, bf16[256,1024]{1,0:T(8,128)(2,1)}, u32[]{:S(2)}, u32[]{:S(2)}) %collective-permute-start.5) | collective-permute-done | bytes 524320 | tf_op jit(solution)/shard_map/cond/branch_1_fun/ppermute | solution.py:438
  243.3 1.5 copy-done
  244.8 7.4 %branch_1_fun.7 = bf16[4,32,2,16,256]{4,3,2,1,0:T(8,128)(2,1)} custom-call(s32[128]{0:T(128)} %add.288.target, s32[1]{0:T(128)} %bitcast.3.group, bf16[128,5,16,128]{3,2,1,0:T(8,128)(2,1)} %copy-done, bf16[256,1024]{1,0:T(8,128)(2,1)S(1)} %copy-done.2, bf16[256,1024]{1,0:T(8,128)(2,1)} %collective-permute-done.3.w1, ...), custom_call_target="tpu_custom_call" | custom-call | tf_op jit(solution)/shard_map/cond/branch_1_fun/pallas_call | solution.py:405
  252.2 29.6 %all_to_all.41 = bf16[4,32,2,16,256]{4,3,2,1,0:T(8,128)(2,1)S(1)} all-to-all(bf16[4,32,2,16,256]{4,3,2,1,0:T(8,128)(2,1)} %branch_1_fun.7), channel_id=1, replica_groups=mesh['seq'=32,'head'=4] {'head'}, dimensions={0} | all-to-all | bytes 4194304 | tf_op jit(solution)/shard_map/cond/branch_1_fun/all_to_all | solution.py:430
  281.8 0.3 copy.31
  282.3 1.3 copy-done.3
  (26 shorter events, 0.7 us)
Async XLA Ops:
  1.3 15.5 %all-to-all-start.8 = ((s32[32,1,32]{2,1,0:T(1,128)}), s32[32,1,32]{2,1,0:T(1,128)S(1)}, u32[]{:S(2)}, u32[]{:S(2)}) async-start(s32[32,1,32]{2,1,0:T(1,128)} %broadcast_in_dim.98), calls=%async_computation.8 | async-start | bytes 32768 | tf_op jit(solution)/shard_map/all_to_all | solution.py:25
  76.2 63.1 %all-to-all-start.5 = ((bf16[32,3,192,128]{3,2,1,0:T(8,128)(2,1)}), bf16[32,3,192,128]{3,2,1,0:T(8,128)(2,1)}, u32[]{:S(2)}, u32[]{:S(2)}) async-start(bf16[32,3,192,128]{3,2,1,0:T(8,128)(2,1)} %get-tuple-element.55), calls=%async_computation.5 | async-start | bytes 9437184 | tf_op jit(solution)/shard_map/cond/branch_1_fun/all_to_all | solution.py:430
  81.7 1.8 copy-start.8
  173.1 15.6 %copy-start.2 = (bf16[256,1024]{1,0:T(8,128)(2,1)S(1)}, bf16[256,1024]{1,0:T(8,128)(2,1)}, u32[]{:S(2)}) copy-start(bf16[256,1024]{1,0:T(8,128)(2,1)} %get-tuple-element.96.w0) | copy-start | bytes 1572868 | tf_op jit(solution)/shard_map/cond
  173.1 70.2 %all-to-all-start.6 = ((bf16[128,5,16,128]{3,2,1,0:T(8,128)(2,1)}), bf16[128,5,16,128]{3,2,1,0:T(8,128)(2,1)S(1)}, u32[]{:S(2)}, u32[]{:S(2)}) async-start(bf16[128,5,16,128]{3,2,1,0:T(8,128)(2,1)} %branch_1_fun.6), calls=%async_computation.6 | async-start | bytes 5242880 | tf_op jit(solution)/shard_map/cond/branch_1_fun/all_to_all | solution.py:430
  188.7 41.3 %collective-permute-start.3 = (bf16[256,1024]{1,0:T(8,128)(2,1)S(1)}, bf16[256,1024]{1,0:T(8,128)(2,1)}, u32[]{:S(2)}, u32[]{:S(2)}) collective-permute-start(bf16[256,1024]{1,0:T(8,128)(2,1)S(1)} %copy-done.2), channel_id=1, source_target_pairs={{1,0},{2,1},{3,2},{0,3},{5,4},{6,5},{7,6},{4,7},{9,8},{10,9},{11,1... | collective-permute-start | bytes 1572872 | tf_op jit(solution)/shard_map/cond/branch_1_fun/ppermute | solution.py:438
  192.0 40.7 %collective-permute-start.4 = (bf16[256,1024]{1,0:T(8,128)(2,1)S(1)}, bf16[256,1024]{1,0:T(8,128)(2,1)}, u32[]{:S(2)}, u32[]{:S(2)}) collective-permute-start(bf16[256,1024]{1,0:T(8,128)(2,1)S(1)} %copy-done.2), channel_id=1, source_target_pairs={{2,0},{3,1},{0,2},{1,3},{6,4},{7,5},{4,6},{5,7},{10,8},{11,9},{8,1... | collective-permute-start | bytes 1572872 | tf_op jit(solution)/shard_map/cond/branch_1_fun/ppermute | solution.py:438
  192.1 51.2 %collective-permute-start.5 = (bf16[256,1024]{1,0:T(8,128)(2,1)S(1)}, bf16[256,1024]{1,0:T(8,128)(2,1)}, u32[]{:S(2)}, u32[]{:S(2)}) collective-permute-start(bf16[256,1024]{1,0:T(8,128)(2,1)S(1)} %copy-done.2), channel_id=1, source_target_pairs={{3,0},{0,1},{1,2},{2,3},{7,4},{4,5},{5,6},{6,7},{11,8},{8,9},{9,10... | collective-permute-start | bytes 1572872 | tf_op jit(solution)/shard_map/cond/branch_1_fun/ppermute | solution.py:438
  243.3 1.5 copy-start
  282.3 1.3 copy-start.3
